TPU v7x, 256 devices: a whole 4x4x8 slice. The times are simulated.
256 devices in a mesh: tile: 128 (over x, z, y), frame: 2 (over core).
Axes of the slice: x: 4, y: 4, z: 8, core: 2. Of those that a mesh axis runs over, the one named last changes fastest.
Arguments:
- movie_block: bfloat16 [128, 8192, 512], P('frame', 'tile'), may hold values from 0 to 0.19921875
- patches: bfloat16 [4096, 64, 64], P('tile'), may hold values from 0.0049743652 to 0.049804688
- patch_rows: int32 [4096], P('tile'), may hold values from -32 to 31
- patch_cols: int32 [4096], P('tile'), may hold values from 0 to 63
- neuron_live: int32 [4096], P('tile'), may hold values from 0 to 1
- neuron_colour: int32 [4096], replicated, may hold values from 0 to 15, as said below
- traces: float32 [4096, 128], P('tile', 'frame'), may hold values from 0.2 to 2
Outputs:
- new_traces: float32 [4096, 128], P('tile', 'frame')
- new_patches: bfloat16 [4096, 64, 64], P('tile')
Inputs may be any that keep to these rules, and one draw needn't show every extreme that they name: `neuron_colour`: slots of one colour never share a pixel: within one tile and column bin every slot has its own colour, and the colours of a bin in a tile and in an adjacent tile are disjoint.
All inputs are finite; a program needn't handle non-finite values.
Results may differ from a plain program's by a relative error of at most 0.005.
Values may be sent and summed in bfloat16 or wider, within the bound.
No kernel may reach another device: no remote copies, remote signals or barrier semaphores. Data moves between devices by JAX's collectives and lax.ppermute only.
A program may use at most 64 MiB of HBM per device.

v0:
```python
import functools

import jax
import jax.numpy as jnp
from jax import lax
from jax.experimental import pallas as pl
from jax.experimental.pallas import tpu as pltpu
from jax.sharding import PartitionSpec as P

exact = lax.Precision.HIGHEST
f32 = jnp.float32
bf16 = jnp.bfloat16
BINS = 4
LAYERS = 8
SLOTS = 32
COLOURS = 16
PATCH = 64
HALF = 32
EDGE = 128
FRAMES = 128
GROUP = BINS * COLOURS
floor_share = 0.25

vmem = pl.BlockSpec(memory_space=pltpu.VMEM)
smem = pl.BlockSpec(memory_space=pltpu.SMEM)


def iota(shape, dim):
    return lax.broadcasted_iota(jnp.int32, shape, dim)


def dot_nt(a, b, precision=None):
    return lax.dot_general(
        a, b, (((1,), (1,)), ((), ())), precision=precision, preferred_element_type=f32
    )


def dot(a, b, precision=None):
    return lax.dot_general(
        a, b, (((1,), (0,)), ((), ())), precision=precision, preferred_element_type=f32
    )


def neighbour_tile(tile, core, tiles):
    other = jnp.where(core == 0, tile - 1, tile + 1)
    other = jnp.where(other < 0, tile + 1, other)
    return jnp.where(other >= tiles, tile - 1, other)


def slab_kernel(
    rows_ref, cols_ref, live_ref, patches_ref, out_ref, own_ref, raw_ref, pad_ref, sems,
):
    core = lax.axis_index("frame")
    chunk = SLOTS // 4
    fetches = []
    for i in range(4):
        part = slice(i * chunk, (i + 1) * chunk)
        fetches.append(pltpu.make_async_copy(patches_ref.at[part], raw_ref.at[part], sems.at[i]))
        fetches[i].start()
    zeros = jnp.zeros((PATCH, EDGE), f32)
    blank = jnp.zeros((PATCH, PATCH), f32)
    for s in range(SLOTS):
        pad_ref[s, :PATCH, :] = zeros
        pad_ref[s, 2 * PATCH :, :] = zeros
    for s in range(SLOTS):
        if s % chunk == 0:
            fetches[s // chunk].wait()
        filled = jnp.where(live_ref[s] > 0, raw_ref[s].astype(f32), 0.0)
        pad_ref[s, PATCH : 2 * PATCH, :] = jnp.concatenate([filled, blank], axis=1)
        start = jnp.where(core == 0, HALF, PATCH + HALF) - rows_ref[s]
        window = pad_ref[s, pl.ds(start, PATCH), :]
        window = pltpu.roll(window, cols_ref[s], 1).astype(bf16)
        upper, lower = window[:HALF], window[HALF:]
        out_ref[s] = jnp.where(core == 0, upper, lower)
        own_ref[s] = jnp.where(core == 0, lower, upper)


def fetch_kernel(live_ref, traces_ref, movie_ref, begin_ref, strip_ref, sems):
    first = pl.multiple_of(HALF * lax.axis_index("frame"), HALF)
    fetches = fetch_rows(movie_ref, strip_ref, first, sems)
    for s in range(SLOTS):
        begin_ref[s : s + 1, :] = traces_ref[s : s + 1, :] * live_ref[s].astype(f32)
    for fetch in fetches:
        fetch.wait()


def table_kernel(colour_ref, anchor_ref, phase_ref, repeat_ref, count_ref, owner_ref):
    tile = lax.axis_index("tile")
    for i in range(GROUP):
        owner_ref[i] = 0
    for s in range(SLOTS):
        at = (s // LAYERS) * COLOURS + colour_ref[tile * SLOTS + s]
        owner_ref[at] = 1
    most = jnp.int32(0)
    for b in range(BINS):
        phase = jnp.int32(0)
        for g in range(COLOURS):
            i = b * COLOURS + g
            if g:
                phase = phase + jnp.abs(owner_ref[i] - owner_ref[i - 1])
            value = phase + 100 * (1 - owner_ref[i])
            phase_ref[i : i + 1, :] = jnp.full((1, FRAMES), value, jnp.int32)
        most = jnp.maximum(most, phase + 1)
    count_ref[0] = most
    position = (iota((FRAMES, 1024), 1) // 8 + 64 * lax.axis_index("frame")) % FRAMES
    repeat_ref[...] = jnp.where(position == iota((FRAMES, 1024), 0), 1.0, 0.0).astype(bf16)


def fetch_rows(movie_ref, strip_ref, first, sems):
    fetches = []
    for i in range(8):
        part = slice(8 * i, 8 * i + 8)
        rows = movie_ref.at[part, pl.ds(first, HALF), :]
        fetches.append(pltpu.make_async_copy(rows, strip_ref.at[part], sems.at[i]))
        fetches[-1].start()
    return fetches


def strips(ref, items, first, lanes):
    parts = []
    for q in range(HALF // 8):
        part = ref[items, pl.ds(pl.multiple_of(first + 8 * q, 8), 8), lanes]
        parts.append(part.reshape(part.shape[0] * 8, EDGE))
    return jnp.concatenate(parts, axis=1)


def partial_kernel(
    tiles, colour_ref, mine_ref, other_ref, own_ref, recv_ref, near_ref, far_ref,
    slab_ref, message_ref, kept_ref, *refs
):
    pixels_refs, (laid_ref, sems) = refs[:BINS], refs[BINS:]
    tile = lax.axis_index("tile")
    core = lax.axis_index("frame")
    beside = neighbour_tile(tile, core, tiles)
    message_ref[...] = jnp.zeros_like(message_ref)
    start = GROUP + COLOURS
    wide = jnp.concatenate([near_ref[...], far_ref[...]], axis=1)
    swapped = jnp.concatenate([far_ref[...], near_ref[...]], axis=1)
    first = jnp.where(core == 0, wide, swapped)
    for s in range(SLOTS):
        b = s // LAYERS
        mine = b * COLOURS + colour_ref[tile * SLOTS + s]
        theirs = b * COLOURS + colour_ref[beside * SLOTS + s]
        slab_ref[mine] = own_ref[s]
        slab_ref[theirs] = recv_ref[s]
        message_ref[pl.ds(start + mine, 1), :] = first[s : s + 1]
    same_row = iota((512, 128), 0) % 8 == iota((512, 128), 1) % 8
    fold = jnp.where(iota((COLOURS, 384), 1) % 128 // 8 == iota((COLOURS, 384), 0), 1.0, 0.0)
    parts = {}
    grams = []
    keeps = []
    boths = []
    for i, ref in enumerate((mine_ref, other_ref)):
        for b in range(BINS):
            if i == 0:
                both = strips(slab_ref, slice(b * COLOURS, (b + 1) * COLOURS), 0, slice(0, EDGE))
                boths.append(both)
                square = jnp.where(same_row[:128], dot_nt(both, both), 0.0)
                grams.append(jnp.sum(square.reshape(COLOURS, 8, 128), axis=1))
            pixels = strips(ref, slice(0, 64), i * HALF * core, slice(b * EDGE, (b + 1) * EDGE))
            if i == 0:
                laid_ref[b] = pixels
                keeps.append(pltpu.make_async_copy(laid_ref.at[b], kept_ref.at[b], sems.at[b]))
                keeps[-1].start()
            else:
                pixels_refs[b][...] = pixels
            product = jnp.where(same_row, dot_nt(pixels, boths[b]), 0.0)
            parts[b, i] = jnp.sum(product.reshape(64, 8, 128), axis=1)
    drives = []
    for b in range(BINS):
        near = jnp.concatenate([parts[b, 0], parts[b, 1]], axis=0)
        far = jnp.concatenate([parts[b, 1], parts[b, 0]], axis=0)
        drives.append(jnp.where(core == 0, near, far))
    drive = dot_nt(fold.astype(bf16), three_parts(jnp.concatenate(drives, axis=0)))
    for b in range(BINS):
        message_ref[b * COLOURS : (b + 1) * COLOURS, :] = drive[:, b * FRAMES : (b + 1) * FRAMES]
    spread = jnp.where(iota((384, EDGE), 0) % 128 // 8 == iota((384, EDGE), 1) % 16, 1.0, 0.0)
    gram = dot(three_parts(jnp.concatenate(grams, axis=0)), spread.astype(bf16))
    lane = iota((COLOURS, EDGE), 1) // COLOURS
    total = jnp.zeros((COLOURS, EDGE), f32)
    for b in range(BINS):
        total = jnp.where(lane == b, gram[b * COLOURS : (b + 1) * COLOURS], total)
    message_ref[GROUP : GROUP + COLOURS, :] = total
    for keep in keeps:
        keep.wait()


def three_parts(value):
    high = value.astype(bf16)
    rest = value - high.astype(f32)
    middle = rest.astype(bf16)
    low = (rest - middle.astype(f32)).astype(bf16)
    return jnp.concatenate([high, middle, low], axis=1)


def block_diagonal(gram):
    tall = jnp.concatenate([gram] * BINS, axis=0)[:, :GROUP]
    keep = iota((GROUP, GROUP), 0) // COLOURS == iota((GROUP, GROUP), 1) // COLOURS
    return jnp.where(keep, tall, 0.0)


def settle(phase_ref, live_ref, gram, residual, current, phase, state_ref, change_ref):
    whole = jnp.concatenate([gram] * BINS, axis=0)
    lane = iota((GROUP, EDGE), 1)
    diag = jnp.sum(jnp.where(lane == iota((GROUP, EDGE), 0), whole, 0.0), axis=1, keepdims=True)
    inverse = 1.0 / (diag + (1.0 - live_ref[...]))
    chosen = phase_ref[...] == phase
    news = []
    changes = []
    for b in range(BINS):
        rows = slice(b * COLOURS, (b + 1) * COLOURS)
        rest, now = residual[rows], current[rows]
        inv, pick = inverse[rows], chosen[rows]
        row_id = iota((COLOURS, FRAMES), 0)
        change = jnp.zeros((COLOURS, FRAMES), f32)
        for g in range(COLOURS):
            at = slice(g, g + 1)
            value = jnp.maximum(now[at] + rest[at] * inv[at], 0.0) - now[at]
            delta = jnp.where(pick[at], value, 0.0)
            lane_at = slice(b * COLOURS + g, b * COLOURS + g + 1)
            column = jnp.broadcast_to(gram[:, lane_at], (COLOURS, FRAMES))
            rest = rest - column * delta
            change = jnp.where(row_id == g, delta, change)
        state_ref[rows, :] = rest
        state_ref[GROUP + b * COLOURS : GROUP + (b + 1) * COLOURS, :] = now + change
        change_ref[rows, :] = change


def pack_kernel(mine_ref, far_ref, out_ref):
    out_ref[:GROUP, :] = mine_ref[:GROUP, :]
    out_ref[GROUP : 2 * GROUP, :] = far_ref[:GROUP, :]
    grams = slice(GROUP, GROUP + COLOURS)
    out_ref[2 * GROUP : 2 * GROUP + COLOURS, :] = mine_ref[grams, :]
    out_ref[2 * GROUP + COLOURS : 2 * GROUP + 2 * COLOURS, :] = far_ref[grams, :]
    out_ref[2 * GROUP + 2 * COLOURS :, :] = mine_ref[GROUP + COLOURS :, :]


near_drive = slice(0, GROUP)
far_drive = slice(GROUP, 2 * GROUP)
near_gram = slice(2 * GROUP, 2 * GROUP + COLOURS)
far_gram = slice(2 * GROUP + COLOURS, 2 * GROUP + 2 * COLOURS)
all_traces = slice(2 * GROUP + 2 * COLOURS, 3 * GROUP + 2 * COLOURS)
PACKED = 3 * GROUP + 2 * COLOURS


def forward_kernel(tiles, pack_ref, pair_ref, anchor_ref, out_ref):
    tile = lax.axis_index("tile")
    core = lax.axis_index("frame")
    last = ((tile == 0) & (core == 0)) | ((tile == tiles - 1) & (core == 1))
    alone = jnp.where(last, 1.0, 0.0)
    out_ref[near_drive, :] = pack_ref[near_drive, :] + pair_ref[near_drive, :]
    out_ref[far_drive, :] = pair_ref[far_drive, :] + alone * pack_ref[far_drive, :]
    out_ref[near_gram, :] = pack_ref[near_gram, :] + pair_ref[near_gram, :]
    out_ref[far_gram, :] = pair_ref[far_gram, :] + alone * pack_ref[far_gram, :]
    out_ref[all_traces, :] = pack_ref[all_traces, :] + pair_ref[all_traces, :]


side_drives = [slice(i * GROUP, (i + 1) * GROUP) for i in range(3)]
side_grams = [slice(3 * GROUP + i * COLOURS, 3 * GROUP + (i + 1) * COLOURS) for i in range(3)]
side_next = slice(3 * GROUP + 3 * COLOURS, 4 * GROUP + 3 * COLOURS)
side_beyond = slice(4 * GROUP + 3 * COLOURS, 5 * GROUP + 3 * COLOURS)
SIDE = 5 * GROUP + 3 * COLOURS


def side_kernel(pack_ref, pair_ref, beyond_ref, out_ref):
    out_ref[side_drives[0], :] = pack_ref[near_drive, :] + pair_ref[near_drive, :]
    out_ref[side_drives[1], :] = pair_ref[far_drive, :] + beyond_ref[far_drive, :]
    out_ref[side_drives[2], :] = beyond_ref[near_drive, :]
    out_ref[side_grams[0], :] = pack_ref[near_gram, :] + pair_ref[near_gram, :]
    out_ref[side_grams[1], :] = pair_ref[far_gram, :] + beyond_ref[far_gram, :]
    out_ref[side_grams[2], :] = beyond_ref[near_gram, :]
    out_ref[side_next, :] = pair_ref[all_traces, :]
    out_ref[side_beyond, :] = beyond_ref[all_traces, :]


def settler(gram):
    whole = jnp.concatenate([gram] * BINS, axis=0)
    diag = jnp.where(iota((GROUP, EDGE), 1) == iota((GROUP, EDGE), 0), whole, 0.0)
    diag = jnp.sum(diag, axis=1, keepdims=True)
    inverse = jnp.broadcast_to(1.0 / jnp.where(diag > 0.0, diag, 1.0), (GROUP, FRAMES))
    row_id = iota((COLOURS, FRAMES), 0)

    def settle(residual, current, chosen):
        rests, changes = [], []
        for b in range(BINS):
            rows = slice(b * COLOURS, (b + 1) * COLOURS)
            rest, now, inv, pick = residual[rows], current[rows], inverse[rows], chosen[rows]
            change = jnp.zeros((COLOURS, FRAMES), f32)
            for g in range(COLOURS):
                at = slice(g, g + 1)
                value = jnp.maximum(now[at] + rest[at] * inv[at], 0.0) - now[at]
                delta = jnp.where(pick[at], value, 0.0)
                lane_at = slice(b * COLOURS + g, b * COLOURS + g + 1)
                rest = rest - jnp.broadcast_to(gram[:, lane_at], (COLOURS, FRAMES)) * delta
                change = jnp.where(row_id == g, delta, change)
            rests.append(rest)
            changes.append(change)
        return jnp.concatenate(rests, axis=0), jnp.concatenate(changes, axis=0)

    return settle


def window_kernel(
    phase_ref, pack_ref, here_ref, there_ref, state_ref, change_ref, gram_ref, before_ref, beside_ref
):
    phase = phase_ref[...]
    own = phase < 100
    start = pack_ref[all_traces, :]
    sides = []
    for ref in (here_ref, there_ref):
        grams = [ref[at, :] for at in side_grams]
        near, beyond = ref[side_next, :], ref[side_beyond, :]
        second = jnp.where(own, beyond, 0.0)
        blocks = [block_diagonal(gram) for gram in grams]
        held = [start + near, near + second, beyond]
        parts = [ref[side_drives[i], :] - dot(blocks[i], held[i], exact) for i in range(3)]
        sides.append((grams, blocks, parts, near, second))
    (grams_a, blocks_a, parts_a, near_a, second_a), (grams_b, blocks_b, parts_b, near_b, second_b) = sides
    mine_now, theirs_now = phase == 0, phase == 100
    settle_own = settler(grams_a[0] + grams_b[0])
    settle_near = settler(grams_a[0] + grams_a[1])
    rest, change = settle_own(parts_a[0] + parts_b[0], start, mine_now)
    rest_a, near_change_a = settle_near(parts_a[0] + parts_a[1], near_a, theirs_now)
    _, near_change_b = settler(grams_b[0] + grams_b[1])(parts_b[0] + parts_b[1], near_b, theirs_now)
    _, second_change = settler(grams_a[1] + grams_a[2])(parts_a[1] + parts_a[2], second_a, mine_now)
    rest = rest - dot(blocks_a[0], near_change_a, exact) - dot(blocks_b[0], near_change_b, exact)
    rest_a = rest_a - dot(blocks_a[0], change, exact) - dot(blocks_a[1], second_change, exact)
    now = start + change
    near_now = near_a + near_change_a
    rest, late = settle_own(rest, now, phase == 1)
    _, near_late = settle_near(rest_a, near_now, phase == 101)
    state_ref[:GROUP, :] = rest
    state_ref[GROUP:, :] = now + late
    change_ref[...] = late
    gram_ref[:COLOURS, :] = grams_a[0]
    gram_ref[COLOURS:, :] = grams_b[0]
    before_ref[...] = near_now
    beside_ref[...] = near_now + near_late


def next_phase_kernel(
    step_ref, phase_ref, gram_ref, old_ref, before_ref, delta_ref, far_delta_ref,
    state_ref, change_ref, before_out_ref,
):
    here = gram_ref[:COLOURS, :]
    there = gram_ref[COLOURS:, :]
    coupled = dot(block_diagonal(here), delta_ref[...], exact)
    coupled = coupled + dot(block_diagonal(there), far_delta_ref[...], exact)
    now = old_ref[GROUP:, :]
    chosen = phase_ref[...] == step_ref[0]
    rest, change = settler(here + there)(old_ref[:GROUP, :] - coupled, now, chosen)
    state_ref[:GROUP, :] = rest
    state_ref[GROUP:, :] = now + change
    change_ref[...] = change
    before_out_ref[...] = before_ref[...] + delta_ref[...]


def spatial_kernel(
    tiles, colour_ref, repeat_ref, *refs
):
    far_refs, refs = refs[:BINS], refs[BINS:]
    kept_ref, slab_ref, state_in_ref, beside_ref, out_ref, own_ref = refs[:6]
    weight_ref, cross_ref, field_ref, state_ref, near_ref, sems = refs[6:]
    fetches = []
    for b in range(BINS):
        fetches.append(pltpu.make_async_copy(kept_ref.at[b], near_ref.at[b], sems.at[b]))
        fetches[-1].start()
    tile = lax.axis_index("tile")
    core = lax.axis_index("frame")
    beside = neighbour_tile(tile, core, tiles)
    both = state_in_ref[GROUP:, :] + beside_ref[...]
    repeated = dot(both.astype(bf16), repeat_ref[...])
    same_row = iota((8, 1024), 0) == iota((8, 1024), 1) % 8
    for b in range(BINS):
        for g in range(0, COLOURS, 2):
            pair = []
            for i in range(2):
                line = repeated[b * COLOURS + g + i : b * COLOURS + g + i + 1]
                pair.append(jnp.where(same_row, line, 0.0))
            weight_ref[b, 8 * g : 8 * g + 16, :] = jnp.concatenate(pair, axis=0).astype(bf16)
        field_ref[b] = dot(weight_ref[b, :, 512:], far_refs[b][...])
    for b in range(BINS):
        rows = slice(b * COLOURS, (b + 1) * COLOURS)
        now = both[rows]
        cross = dot_nt(now, now, exact)
        for g in range(COLOURS):
            column = jnp.broadcast_to(cross[:, g : g + 1], (COLOURS, EDGE))
            cross_ref[(b * COLOURS + g) * 16 : (b * COLOURS + g) * 16 + 16, :] = column
    for b in range(BINS):
        fetches[b].wait()
        field_ref[b] = field_ref[b] + dot(weight_ref[b, :, :512], near_ref[b])

    floor = floor_share * FRAMES

    def update(step, carry):
        b = step // 2
        q = step % 2
        first = b * COLOURS
        row = pl.multiple_of(q * 16, 16)
        states = [
            slab_ref[first + m, pl.ds(row, 16), :].astype(f32) for m in range(COLOURS)
        ]
        for g in range(COLOURS):
            base = (first + g) * 16
            support = states[g] > 0.0
            field = jnp.concatenate(
                [
                    field_ref[b, 8 * g : 8 * g + 8, pl.ds(pl.multiple_of((2 * q + i) * EDGE, EDGE), EDGE)]
                    for i in range(2)
                ],
                axis=0,
            )
            rest = field
            for m in list(range(g, COLOURS)) + list(range(g)):
                rest = rest - cross_ref[pl.ds(base + m, 1), :] * states[m]
            scale = 1.0 / jnp.maximum(cross_ref[pl.ds(base + g, 1), :], floor)
            fresh = jnp.maximum(states[g] + rest * scale, 0.0)
            fresh = jnp.where(support, fresh, 0.0).astype(bf16)
            state_ref[first + g, pl.ds(row, 16), :] = fresh
            states[g] = fresh.astype(f32)
        return carry

    lax.fori_loop(0, 2 * BINS, update, 0)
    for s in range(SLOTS):
        first = (s // LAYERS) * COLOURS
        own_ref[s] = state_ref[first + colour_ref[tile * SLOTS + s]]
        out_ref[s] = state_ref[first + colour_ref[beside * SLOTS + s]]


def patch_kernel(
    rows_ref, cols_ref, colour_ref, state_ref, own_ref, recv_ref, sib_own_ref, sib_recv_ref,
    out_ref, traces_ref, framed_ref,
):
    tile = lax.axis_index("tile")
    own = state_ref[GROUP:, :]
    rolled = jnp.concatenate([own[:, 64:], own[:, :64]], axis=1)
    framed_ref[...] = jnp.where(lax.axis_index("frame") == 0, own, rolled)[:, :64]
    core = lax.axis_index("frame")
    line = iota((PATCH, EDGE), 1)
    block = line // HALF
    home = jnp.where(core == 0, HALF, 2 * HALF)
    edge = jnp.where(core == 0, 0, 3 * HALF)
    far_home = 3 * HALF - home
    far_edge = 3 * HALF - edge
    base = jnp.where(block == 0, home, jnp.where(block == 1, edge, jnp.where(block == 2, far_home, far_edge)))
    row_at = base + line % HALF - HALF - iota((PATCH, EDGE), 0)
    col_at = iota((EDGE, PATCH), 0) - iota((EDGE, PATCH), 1)
    for s in range(SLOTS):
        at = (s // LAYERS) * COLOURS + colour_ref[tile * SLOTS + s]
        traces_ref[s : s + 1, :] = framed_ref[pl.ds(at, 1), :]
        row_pick = jnp.where(row_at == rows_ref[s], 1.0, 0.0).astype(bf16)
        col_pick = jnp.where(col_at == cols_ref[s], 1.0, 0.0).astype(bf16)
        whole = jnp.concatenate([own_ref[s], recv_ref[s], sib_own_ref[s], sib_recv_ref[s]], axis=0)
        lifted = dot(row_pick, whole).astype(bf16)
        out_ref[s] = dot(lifted, col_pick).astype(bf16)


def shape(dims, dtype=f32):
    return jax.ShapeDtypeStruct(dims, dtype)


def call(kernel, ins, outs, name, limit, scratch=(), out_specs=None):
    return pl.pallas_call(
        kernel,
        in_specs=ins,
        out_specs=out_specs or [vmem] * len(outs),
        out_shape=outs,
        scratch_shapes=list(scratch),
        name=name,
        compiler_params=pltpu.CompilerParams(vmem_limit_bytes=limit * 2**20),
    )


def on_device(movie_block, patches, patch_rows, patch_cols, neuron_live, neuron_colour, traces):
    tiles = lax.axis_size("tile")
    swap_pairs = []
    for t in range(tiles - 1):
        swap_pairs += [(2 * t + 1, 2 * t + 2), (2 * t + 2, 2 * t + 1)]

    def pair_swap(value):
        return lax.ppermute(value, ("tile", "frame"), swap_pairs)

    far_pairs = [(2 * (tiles - 1) + 1, 2 * (tiles - 3) + 1), (0, 4)]
    for t in range(tiles - 3):
        far_pairs += [(2 * t + 1, 2 * (t + 3)), (2 * (t + 3), 2 * t + 1)]

    def chip_swap(value):
        return lax.ppermute(value, "frame", [(0, 1), (1, 0)])

    def in_hbm(value):
        return pltpu.with_memory_space_constraint(value, pltpu.HBM)

    piece = shape((SLOTS, HALF, EDGE), bf16)
    group = shape((GROUP, FRAMES))
    hbm = pl.BlockSpec(memory_space=pltpu.HBM)
    movie_far = chip_swap(movie_block)
    piece_out, piece_own = call(
        slab_kernel,
        [smem, smem, smem, hbm],
        [piece, piece],
        "slabs",
        8,
        [
            pltpu.VMEM((SLOTS, PATCH, PATCH), bf16),
            pltpu.VMEM((SLOTS, 3 * PATCH, EDGE), f32),
            pltpu.SemaphoreType.DMA((4,)),
        ],
    )(in_hbm(patch_rows), in_hbm(patch_cols), in_hbm(neuron_live), in_hbm(patches))
    piece_recv = pair_swap(piece_out)
    begin, movie_strip = call(
        fetch_kernel,
        [smem, vmem, hbm],
        [shape((SLOTS, 64)), shape((64, HALF, 512), bf16)],
        "fetch",
        4,
        [pltpu.SemaphoreType.DMA((8,))],
    )(in_hbm(neuron_live), in_hbm(traces), in_hbm(movie_block))
    begin_far = chip_swap(begin)

    slab, message, kept, *far_pixels = call(
        functools.partial(partial_kernel, tiles),
        [smem] + [vmem] * 6,
        [
            shape((GROUP, HALF, EDGE), bf16), shape((2 * GROUP + COLOURS, FRAMES)),
            pltpu.HBM((BINS, 512, 512), bf16),
        ]
        + [shape((512, 512), bf16)] * BINS,
        "partial_sums",
        12,
        [pltpu.VMEM((BINS, 512, 512), bf16), pltpu.SemaphoreType.DMA((BINS,))],
        [vmem, vmem, hbm] + [vmem] * BINS,
    )(neuron_colour, movie_strip, movie_far, piece_own, piece_recv, begin, begin_far)

    packed_shape, side_shape = shape((PACKED, FRAMES)), shape((SIDE, FRAMES))
    state_shape = shape((2 * GROUP, FRAMES))
    (packed,) = call(pack_kernel, [vmem] * 2, [packed_shape], "pack", 2)(message, chip_swap(message))
    pair = pair_swap(packed)
    phases, repeat, phase_count = call(
        table_kernel,
        [smem, vmem],
        [shape((GROUP, FRAMES), jnp.int32), shape((FRAMES, 1024), bf16), shape((1,), jnp.int32)],
        "tables",
        2,
        [pltpu.SMEM((GROUP,), jnp.int32)],
        [vmem, vmem, smem],
    )(neuron_colour, packed)
    (onward,) = call(
        functools.partial(forward_kernel, tiles), [vmem] * 3, [packed_shape], "forward", 2
    )(packed, pair, phases)
    beyond = lax.ppermute(onward, ("tile", "frame"), far_pairs)
    (side,) = call(side_kernel, [vmem] * 3, [side_shape], "side", 2)(packed, pair, beyond)
    state, change, gram, before, beside = call(
        window_kernel,
        [vmem] * 4,
        [state_shape, group, shape((2 * COLOURS, FRAMES)), group, group],
        "window",
        8,
    )(phases, packed, side, chip_swap(side))

    def advance(carry):
        step, state, before, change, _ = carry
        delta = pair_swap(change)
        state, change, before = call(
            next_phase_kernel, [smem] + [vmem] * 6, [state_shape, group, group], "next_phase", 4
        )(step.reshape(1), phases, gram, state, before, delta, chip_swap(delta))
        return step + 1, state, before, change, before + pair_swap(change)

    carry = (jnp.int32(2), state, before, change, beside)
    _, state, _, _, beside = lax.while_loop(lambda c: c[0] < phase_count[0], advance, carry)

    final_out, final_own = call(
        functools.partial(spatial_kernel, tiles),
        [smem] + [vmem] * 5 + [hbm] + [vmem] * 3,
        [piece, piece],
        "spatial",
        10,
        [
            pltpu.VMEM((BINS, 128, 1024), bf16),
            pltpu.VMEM((GROUP * COLOURS, EDGE), f32),
            pltpu.VMEM((BINS, 128, 512), f32),
            pltpu.VMEM((GROUP, HALF, EDGE), bf16),
            pltpu.VMEM((BINS, 512, 512), bf16),
            pltpu.SemaphoreType.DMA((BINS,)),
        ],
    )(neuron_colour, repeat, *far_pixels, in_hbm(kept), slab, state, beside)

    far_own = chip_swap(final_own)
    final_recv = pair_swap(final_out)
    far_recv = chip_swap(final_recv)
    new_patches, new_traces = call(
        patch_kernel,
        [smem] * 3 + [vmem] * 5,
        [shape((SLOTS, PATCH, PATCH), bf16), shape((SLOTS, 64))],
        "patches",
        8,
        [pltpu.VMEM((GROUP, 64), f32)],
    )(patch_rows, patch_cols, neuron_colour, state, final_own, final_recv, far_own, far_recv)
    return (new_traces, new_patches)


def solution(mesh):
    placed = (
        P("frame", "tile", None),
        P("tile", None, None),
        P("tile"),
        P("tile"),
        P("tile"),
        P(),
        P("tile", "frame"),
    )
    return jax.shard_map(
        on_device,
        mesh=mesh,
        in_specs=placed,
        out_specs=(P("tile", "frame"), P("tile", None, None)),
        check_vma=False,
    )
```

profile of v0, /device:TPU:6, one launch (start us, length us, event | category | flops | bytes accessed | tf_op | source)
XLA Modules:
  0.0 66.9 jit_solution(9538196760342644508)
XLA Ops:
  0.6 0.0 copy-start
  0.6 0.1 collective-permute-start.3
  0.7 2.2 %slabs.1 = (bf16[32,32,128]{2,1,0:T(8,128)(2,1)S(1)}, bf16[32,32,128]{2,1,0:T(8,128)(2,1)S(1)}) custom-call(s32[32]{0:T(128)} %rows_ref.3, s32[32]{0:T(128)} %cols_ref.3, s32[32]{0:T(128)} %live_ref.3, bf16[32,64,64]{2,1,0:T(8,128)(2,1)} %patches_ref.1), custom_call_target="tpu_custom_call" | custom-call | tf_op jit(solution)/shard_map/slabs/pallas_call | solution.py:497
  2.9 10.6 %collective-permute-start.4 = (bf16[32,32,128]{2,1,0:T(8,128)(2,1)S(1)}, bf16[32,32,128]{2,1,0:T(8,128)(2,1)S(1)}, u32[]{:S(2)}, u32[]{:S(2)}) collective-permute-start(bf16[32,32,128]{2,1,0:T(8,128)(2,1)S(1)} %get-tuple-element.73), channel_id=1, source_target_pairs={{1,2},{2,1},{3,4},{4,3},{5,6},{6,5},{7,8},{8,7},{9,10},{10,9},{11,... | collective-permute-start | bytes 786440 | tf_op jit(solution)/shard_map/ppermute | solution.py:481
  13.5 2.3 %fetch.1 = (f32[32,64]{1,0:T(8,128)S(1)}, bf16[64,32,512]{2,1,0:T(8,128)(2,1)S(1)}) custom-call(s32[32]{0:T(128)} %live_ref.3, f32[32,64]{1,0:T(8,128)} %traces_ref.1, bf16[64,64,512]{2,1,0:T(8,128)(2,1)} %movie_ref.1), custom_call_target="tpu_custom_call" | custom-call | tf_op jit(solution)/shard_map/fetch/pallas_call | solution.py:510
  15.9 0.1 collective-permute-start.5
  16.0 1.2 %collective-permute-done.5.far_ref = f32[32,64]{1,0:T(8,128)S(1)} collective-permute-done((f32[32,64]{1,0:T(8,128)S(1)}, f32[32,64]{1,0:T(8,128)S(1)}, u32[]{:S(2)}, u32[]{:S(2)}) %collective-permute-start.5) | collective-permute-done | bytes 8224 | tf_op jit(solution)/shard_map/ppermute | solution.py:488
  17.1 0.5 collective-permute-done.4.recv_ref
  17.6 0.0 collective-permute-done.3.other_ref
  17.6 0.0 copy-done
  17.6 3.9 %partial_sums.1 = (bf16[64,32,128]{2,1,0:T(8,128)(2,1)S(1)}, f32[144,128]{1,0:T(8,128)S(1)}, bf16[4,512,512]{2,1,0:T(8,128)(2,1)}, bf16[512,512]{1,0:T(8,128)(2,...) custom-call(s32[4096]{0:T(1024)S(1)} %copy-done, ...), custom_call_target="tpu_custom_call" | custom-call | tf_op jit(solution)/shard_map/partial_sums/pallas_call | solution.py:520
  21.5 0.1 collective-permute-start.6
  21.6 1.3 %collective-permute-done.6.far_ref = f32[144,128]{1,0:T(8,128)S(1)} collective-permute-done((f32[144,128]{1,0:T(8,128)S(1)}, f32[144,128]{1,0:T(8,128)S(1)}, u32[]{:S(2)}, u32[]{:S(2)}) %collective-permute-start.6) | collective-permute-done | bytes 73760 | tf_op jit(solution)/shard_map/ppermute | solution.py:488
  22.9 7.9 %collective-permute-start.7 = (f32[224,128]{1,0:T(8,128)S(1)}, f32[224,128]{1,0:T(8,128)S(1)}, u32[]{:S(2)}, u32[]{:S(2)}) collective-permute-start(f32[224,128]{1,0:T(8,128)S(1)} %pack.1.anchor_ref.pack_ref), channel_id=1, source_target_pairs={{1,2},{2,1},{3,4},{4,3},{5,6},{6,5},{7,8},{8,7},{9,10},{10,9},{11,... | collective-permute-start | bytes 344072 | tf_op jit(solution)/shard_map/ppermute | solution.py:481
  30.8 1.5 %tables.1 = (s32[64,128]{1,0:T(8,128)S(1)}, bf16[128,1024]{1,0:T(8,128)(2,1)S(1)}, s32[1]{0:T(128)}) custom-call(s32[4096]{0:T(1024)S(1)} %copy-done, f32[224,128]{1,0:T(8,128)S(1)} %pack.1.anchor_ref.pack_ref), custom_call_target="tpu_custom_call" | custom-call | tf_op jit(solution)/shard_map/tables/pallas_call | solution.py:538
  32.3 0.9 %collective-permute-done.7.pair_ref = f32[224,128]{1,0:T(8,128)S(1)} collective-permute-done((f32[224,128]{1,0:T(8,128)S(1)}, f32[224,128]{1,0:T(8,128)S(1)}, u32[]{:S(2)}, u32[]{:S(2)}) %collective-permute-start.7) | collective-permute-done | bytes 114720 | tf_op jit(solution)/shard_map/ppermute | solution.py:481
  33.2 1.9 %collective-permute-start.8 = (f32[224,128]{1,0:T(8,128)S(1)}, f32[224,128]{1,0:T(8,128)S(1)}, u32[]{:S(2)}, u32[]{:S(2)}) collective-permute-start(f32[224,128]{1,0:T(8,128)S(1)} %forward.1), channel_id=1, source_target_pairs={{255,251},{0,4},{1,6},{6,1},{3,8},{8,3},{5,10},{10,5},{7,12},{12,7... | collective-permute-start | bytes 344072 | tf_op jit(solution)/shard_map/ppermute | solution.py:550
  35.2 7.2 %collective-permute-done.8.beyond_ref = f32[224,128]{1,0:T(8,128)S(1)} collective-permute-done((f32[224,128]{1,0:T(8,128)S(1)}, f32[224,128]{1,0:T(8,128)S(1)}, u32[]{:S(2)}, u32[]{:S(2)}) %collective-permute-start.8) | collective-permute-done | bytes 114720 | tf_op jit(solution)/shard_map/ppermute | solution.py:550
  42.4 0.0 copy-start.1
  42.4 0.0 copy-start.2
  42.4 0.1 collective-permute-start.9
  42.5 1.4 %collective-permute-done.9.there_ref = f32[368,128]{1,0:T(8,128)S(1)} collective-permute-done((f32[368,128]{1,0:T(8,128)S(1)}, f32[368,128]{1,0:T(8,128)S(1)}, u32[]{:S(2)}, u32[]{:S(2)}) %collective-permute-start.9) | collective-permute-done | bytes 188448 | tf_op jit(solution)/shard_map/ppermute | solution.py:488
  43.9 2.0 %window.1 = (f32[128,128]{1,0:T(8,128)S(1)}, f32[64,128]{1,0:T(8,128)}, f32[32,128]{1,0:T(8,128)S(1)}, f32[64,128]{1,0:T(8,128)S(1)}, f32[64,128]{1,0:T(8,128)}) custom-call(s32[64,128]{1,0:T(8,128)S(1)} %get-tuple-element.172.anchor_ref.phase_ref, f32[224,128]{1,0:T(8,128)S(1)} %pack.1.anchor_ref.pack_ref, f32[368,128]{1,0:T(8,128)S(1)} %side.1.here_ref, ...), custom_call_target="tpu_custom_call" | custom-call | tf_op jit(solution)/shard_map/window/pallas_call | solution.py:552
  46.0 0.6 while.16
  46.6 4.4 %spatial.1 = (bf16[32,32,128]{2,1,0:T(8,128)(2,1)S(1)}, bf16[32,32,128]{2,1,0:T(8,128)(2,1)S(1)}) custom-call(s32[4096]{0:T(1024)S(1)} %copy-done, bf16[128,1024]{1,0:T(8,128)(2,1)S(1)} %get-tuple-element.84.repeat_ref, bf16[512,512]{1,0:T(8,128)(2,1)S(1)} %get-tuple-element.85.refs_0_, bf16[512,512]{1,0:T(8,128)(2,1)S(1)} %get-tuple-element.86.refs_1_, ...), custom_call_target="tpu_custom_call" | custom-call | tf_op jit(solution)/shard_map/spatial/pallas_call | solution.py:571
  51.0 7.9 %collective-permute-start.10 = (bf16[32,32,128]{2,1,0:T(8,128)(2,1)S(1)}, bf16[32,32,128]{2,1,0:T(8,128)(2,1)S(1)}, u32[]{:S(2)}, u32[]{:S(2)}) collective-permute-start(bf16[32,32,128]{2,1,0:T(8,128)(2,1)S(1)} %get-tuple-element.93), channel_id=1, source_target_pairs={{1,2},{2,1},{3,4},{4,3},{5,6},{6,5},{7,8},{8,7},{9,10},{10,9},{11,... | collective-permute-start | bytes 786440 | tf_op jit(solution)/shard_map/ppermute | solution.py:481
  58.9 0.1 collective-permute-start.11
  59.0 3.9 %collective-permute-done.10.recv_ref = bf16[32,32,128]{2,1,0:T(8,128)(2,1)S(1)} collective-permute-done((bf16[32,32,128]{2,1,0:T(8,128)(2,1)S(1)}, bf16[32,32,128]{2,1,0:T(8,128)(2,1)S(1)}, u32[]{:S(2)}, u32[]{:S(2)}) %collective-permute-start.10) | collective-permute-done | bytes 262176 | tf_op jit(solution)/shard_map/ppermute | solution.py:481
  62.9 0.0 collective-permute-start.12
  62.9 0.0 collective-permute-done.11.sib_own_ref
  62.9 1.5 %collective-permute-done.12.sib_recv_ref = bf16[32,32,128]{2,1,0:T(8,128)(2,1)S(1)} collective-permute-done((bf16[32,32,128]{2,1,0:T(8,128)(2,1)S(1)}, bf16[32,32,128]{2,1,0:T(8,128)(2,1)S(1)}, u32[]{:S(2)}, u32[]{:S(2)}) %collective-permute-start.12) | collective-permute-done | bytes 262176 | tf_op jit(solution)/shard_map/ppermute | solution.py:488
  64.5 0.0 copy-done.1
  64.5 0.0 copy-done.2
  64.5 2.4 %patches.1 = (bf16[32,64,64]{2,1,0:T(8,128)(2,1)}, f32[32,64]{1,0:T(8,128)}) custom-call(s32[32]{0:T(128)S(1)} %copy-done.1, s32[32]{0:T(128)S(1)} %copy-done.2, s32[4096]{0:T(1024)S(1)} %copy-done, f32[128,128]{1,0:T(8,128)S(1)} %get-tuple-element.83.refs_6_.state_ref, bf16[32,32,128]{2,1,0:T(8,128)(2,1)S(1)} %get-tuple-element.92.own_ref, ...), custom_call_target="tpu_custom_call" | custom-call | tf_op jit(solution)/shard_map/patches/pallas_call | solution.py:590
  (3 shorter events, 0.0 us)
Async XLA Ops:
  0.6 17.0 %copy-start = (s32[4096]{0:T(1024)S(1)}, s32[4096]{0:T(1024)}, u32[]{:S(2)}) copy-start(s32[4096]{0:T(1024)} %colour_ref.7) | copy-start | bytes 49156
  0.6 17.0 %collective-permute-start.3 = (bf16[64,64,512]{2,1,0:T(8,128)(2,1)}, bf16[64,64,512]{2,1,0:T(8,128)(2,1)S(1)}, u32[]{:S(2)}, u32[]{:S(2)}) collective-permute-start(bf16[64,64,512]{2,1,0:T(8,128)(2,1)} %movie_ref.1), channel_id=1, source_target_pairs={{0,1},{1,0},{2,3},{3,2},{4,5},{5,4},{6,7},{7,6},{8,9},{9,8},{10,11... | collective-permute-start | bytes 12582920 | tf_op jit(solution)/shard_map/ppermute | solution.py:488
  2.9 14.7 %collective-permute-start.4 = (bf16[32,32,128]{2,1,0:T(8,128)(2,1)S(1)}, bf16[32,32,128]{2,1,0:T(8,128)(2,1)S(1)}, u32[]{:S(2)}, u32[]{:S(2)}) collective-permute-start(bf16[32,32,128]{2,1,0:T(8,128)(2,1)S(1)} %get-tuple-element.73), channel_id=1, source_target_pairs={{1,2},{2,1},{3,4},{4,3},{5,6},{6,5},{7,8},{8,7},{9,10},{10,9},{11,... | collective-permute-start | bytes 786440 | tf_op jit(solution)/shard_map/ppermute | solution.py:481
  15.9 1.3 %collective-permute-start.5 = (f32[32,64]{1,0:T(8,128)S(1)}, f32[32,64]{1,0:T(8,128)S(1)}, u32[]{:S(2)}, u32[]{:S(2)}) collective-permute-start(f32[32,64]{1,0:T(8,128)S(1)} %get-tuple-element.74.near_ref), channel_id=1, source_target_pairs={{0,1},{1,0},{2,3},{3,2},{4,5},{5,4},{6,7},{7,6},{8,9},{9,8},{10,11... | collective-permute-start | bytes 24584 | tf_op jit(solution)/shard_map/ppermute | solution.py:488
  21.5 1.4 %collective-permute-start.6 = (f32[144,128]{1,0:T(8,128)S(1)}, f32[144,128]{1,0:T(8,128)S(1)}, u32[]{:S(2)}, u32[]{:S(2)}) collective-permute-start(f32[144,128]{1,0:T(8,128)S(1)} %get-tuple-element.75.mine_ref), channel_id=1, source_target_pairs={{0,1},{1,0},{2,3},{3,2},{4,5},{5,4},{6,7},{7,6},{8,9},{9,8},{10,11... | collective-permute-start | bytes 221192 | tf_op jit(solution)/shard_map/ppermute | solution.py:488
  22.9 10.3 %collective-permute-start.7 = (f32[224,128]{1,0:T(8,128)S(1)}, f32[224,128]{1,0:T(8,128)S(1)}, u32[]{:S(2)}, u32[]{:S(2)}) collective-permute-start(f32[224,128]{1,0:T(8,128)S(1)} %pack.1.anchor_ref.pack_ref), channel_id=1, source_target_pairs={{1,2},{2,1},{3,4},{4,3},{5,6},{6,5},{7,8},{8,7},{9,10},{10,9},{11,... | collective-permute-start | bytes 344072 | tf_op jit(solution)/shard_map/ppermute | solution.py:481
  33.2 9.1 %collective-permute-start.8 = (f32[224,128]{1,0:T(8,128)S(1)}, f32[224,128]{1,0:T(8,128)S(1)}, u32[]{:S(2)}, u32[]{:S(2)}) collective-permute-start(f32[224,128]{1,0:T(8,128)S(1)} %forward.1), channel_id=1, source_target_pairs={{255,251},{0,4},{1,6},{6,1},{3,8},{8,3},{5,10},{10,5},{7,12},{12,7... | collective-permute-start | bytes 344072 | tf_op jit(solution)/shard_map/ppermute | solution.py:550
  42.4 22.1 %copy-start.1 = (s32[32]{0:T(128)S(1)}, s32[32]{0:T(128)}, u32[]{:S(2)}) copy-start(s32[32]{0:T(128)} %rows_ref.3) | copy-start | bytes 388
  42.4 22.1 %copy-start.2 = (s32[32]{0:T(128)S(1)}, s32[32]{0:T(128)}, u32[]{:S(2)}) copy-start(s32[32]{0:T(128)} %cols_ref.3) | copy-start | bytes 388
  42.4 1.5 %collective-permute-start.9 = (f32[368,128]{1,0:T(8,128)S(1)}, f32[368,128]{1,0:T(8,128)S(1)}, u32[]{:S(2)}, u32[]{:S(2)}) collective-permute-start(f32[368,128]{1,0:T(8,128)S(1)} %side.1.here_ref), channel_id=1, source_target_pairs={{0,1},{1,0},{2,3},{3,2},{4,5},{5,4},{6,7},{7,6},{8,9},{9,8},{10,11... | collective-permute-start | bytes 565256 | tf_op jit(solution)/shard_map/ppermute | solution.py:488
  51.0 11.9 %collective-permute-start.10 = (bf16[32,32,128]{2,1,0:T(8,128)(2,1)S(1)}, bf16[32,32,128]{2,1,0:T(8,128)(2,1)S(1)}, u32[]{:S(2)}, u32[]{:S(2)}) collective-permute-start(bf16[32,32,128]{2,1,0:T(8,128)(2,1)S(1)} %get-tuple-element.93), channel_id=1, source_target_pairs={{1,2},{2,1},{3,4},{4,3},{5,6},{6,5},{7,8},{8,7},{9,10},{10,9},{11,... | collective-permute-start | bytes 786440 | tf_op jit(solution)/shard_map/ppermute | solution.py:481
  58.9 4.0 %collective-permute-start.11 = (bf16[32,32,128]{2,1,0:T(8,128)(2,1)S(1)}, bf16[32,32,128]{2,1,0:T(8,128)(2,1)S(1)}, u32[]{:S(2)}, u32[]{:S(2)}) collective-permute-start(bf16[32,32,128]{2,1,0:T(8,128)(2,1)S(1)} %get-tuple-element.92.own_ref), channel_id=1, source_target_pairs={{0,1},{1,0},{2,3},{3,2},{4,5},{5,4},{6,7},{7,6},{8,9},{9,8},{10,11... | collective-permute-start | bytes 786440 | tf_op jit(solution)/shard_map/ppermute | solution.py:488
  62.9 1.5 %collective-permute-start.12 = (bf16[32,32,128]{2,1,0:T(8,128)(2,1)S(1)}, bf16[32,32,128]{2,1,0:T(8,128)(2,1)S(1)}, u32[]{:S(2)}, u32[]{:S(2)}) collective-permute-start(bf16[32,32,128]{2,1,0:T(8,128)(2,1)S(1)} %collective-permute-done.10.recv_ref), channel_id=1, source_target_pairs={{0,1},{1,0},{2,3},{3,2},{4,5},{5,4},{6,7},{7,6},{8,9},{9,8},{10,11... | collective-permute-start | bytes 786440 | tf_op jit(solution)/shard_map/ppermute | solution.py:488
where the time goes:
time: 67.5 us; the launch traced here: 66.9 us
  starting transfers between devices  28.7 us (43%)
  Pallas kernels  18.8 us (28%)
  waiting for transfers between devices  17.9 us (27%)
  between operations  0.79 us (1%)
    ppermute x3, starting transfers between devices, pair_swap(): return lax.ppermute(value, ('tile', 'frame'), swap_pairs)  26.3 us
    ppermute x1, waiting for transfers between devices, on_device(): beyond = lax.ppermute(onward, ('tile', 'frame'), far_pairs)  7.19 us
    ppermute x6, waiting for transfers between devices, chip_swap(): return lax.ppermute(value, 'frame', [(0, 1), (1, 0)])  5.37 us
    ppermute x3, waiting for transfers between devices, pair_swap(): return lax.ppermute(value, ('tile', 'frame'), swap_pairs)  5.3 us
    pallas_call x1, Pallas kernels, on_device(): call(functools.partial(spatial_kernel, tiles), [smem] + [vmem] * 5 + [hbm...  4.42 us
    pallas_call x1, Pallas kernels, on_device(): call(functools.partial(partial_kernel, tiles), [smem] + [vmem] * 6, [shap...  3.92 us
    pallas_call x1, Pallas kernels, on_device(): call(patch_kernel, [smem] * 3 + [vmem] * 5, [shape((SLOTS, PATCH, PATCH),...  2.39 us
    pallas_call x1, Pallas kernels, on_device(): call(fetch_kernel, [smem, vmem, hbm], [shape((SLOTS, 64)), shape((64, HAL...  2.31 us
  transfers between devices with their start and end apart: 10, of which 8 were waited for; matrix products, arithmetic and copies ran while one was open for 0% of the time, Pallas kernels for 9%

commit v1 on v0

--- a/solution.py
+++ b/solution.py
@@ -101,7 +101,7 @@
             value = phase + 100 * (1 - owner_ref[i])
             phase_ref[i : i + 1, :] = jnp.full((1, FRAMES), value, jnp.int32)
         most = jnp.maximum(most, phase + 1)
-    count_ref[0] = most
+    count_ref[...] = jnp.full((1, 1), most, jnp.int32)
     position = (iota((FRAMES, 1024), 1) // 8 + 64 * lax.axis_index("frame")) % FRAMES
     repeat_ref[...] = jnp.where(position == iota((FRAMES, 1024), 0), 1.0, 0.0).astype(bf16)
 
@@ -126,9 +126,8 @@
 
 def partial_kernel(
     tiles, colour_ref, mine_ref, other_ref, own_ref, recv_ref, near_ref, far_ref,
-    slab_ref, message_ref, kept_ref, *refs
+    slab_ref, message_ref, *pixels_refs,
 ):
-    pixels_refs, (laid_ref, sems) = refs[:BINS], refs[BINS:]
     tile = lax.axis_index("tile")
     core = lax.axis_index("frame")
     beside = neighbour_tile(tile, core, tiles)
@@ -148,7 +147,6 @@
     fold = jnp.where(iota((COLOURS, 384), 1) % 128 // 8 == iota((COLOURS, 384), 0), 1.0, 0.0)
     parts = {}
     grams = []
-    keeps = []
     boths = []
     for i, ref in enumerate((mine_ref, other_ref)):
         for b in range(BINS):
@@ -158,12 +156,7 @@
                 square = jnp.where(same_row[:128], dot_nt(both, both), 0.0)
                 grams.append(jnp.sum(square.reshape(COLOURS, 8, 128), axis=1))
             pixels = strips(ref, slice(0, 64), i * HALF * core, slice(b * EDGE, (b + 1) * EDGE))
-            if i == 0:
-                laid_ref[b] = pixels
-                keeps.append(pltpu.make_async_copy(laid_ref.at[b], kept_ref.at[b], sems.at[b]))
-                keeps[-1].start()
-            else:
-                pixels_refs[b][...] = pixels
+            pixels_refs[b][512 * i : 512 * i + 512, :] = pixels
             product = jnp.where(same_row, dot_nt(pixels, boths[b]), 0.0)
             parts[b, i] = jnp.sum(product.reshape(64, 8, 128), axis=1)
     drives = []
@@ -181,8 +174,6 @@
     for b in range(BINS):
         total = jnp.where(lane == b, gram[b * COLOURS : (b + 1) * COLOURS], total)
     message_ref[GROUP : GROUP + COLOURS, :] = total
-    for keep in keeps:
-        keep.wait()
 
 
 def three_parts(value):
@@ -301,8 +292,10 @@
 
 
 def window_kernel(
-    phase_ref, pack_ref, here_ref, there_ref, state_ref, change_ref, gram_ref, before_ref, beside_ref
+    count_ref, phase_ref, pack_ref, here_ref, there_ref, state_ref, change_ref, gram_ref, before_ref,
+    beside_ref, left_ref,
 ):
+    left_ref[...] = count_ref[...] - 2
     phase = phase_ref[...]
     own = phase < 100
     start = pack_ref[all_traces, :]
@@ -338,16 +331,22 @@
     beside_ref[...] = near_now + near_late
 
 
+def add_kernel(a_ref, b_ref, out_ref):
+    out_ref[...] = a_ref[...] + b_ref[...]
+
+
 def next_phase_kernel(
-    step_ref, phase_ref, gram_ref, old_ref, before_ref, delta_ref, far_delta_ref,
-    state_ref, change_ref, before_out_ref,
+    left_ref, count_ref, phase_ref, gram_ref, old_ref, before_ref, delta_ref, far_delta_ref,
+    state_ref, change_ref, before_out_ref, left_out_ref,
 ):
+    step = count_ref[...] - left_ref[...]
+    left_out_ref[...] = left_ref[...] - 1
     here = gram_ref[:COLOURS, :]
     there = gram_ref[COLOURS:, :]
     coupled = dot(block_diagonal(here), delta_ref[...], exact)
     coupled = coupled + dot(block_diagonal(there), far_delta_ref[...], exact)
     now = old_ref[GROUP:, :]
-    chosen = phase_ref[...] == step_ref[0]
+    chosen = phase_ref[...] == step
     rest, change = settler(here + there)(old_ref[:GROUP, :] - coupled, now, chosen)
     state_ref[:GROUP, :] = rest
     state_ref[GROUP:, :] = now + change
@@ -358,13 +357,9 @@
 def spatial_kernel(
     tiles, colour_ref, repeat_ref, *refs
 ):
-    far_refs, refs = refs[:BINS], refs[BINS:]
-    kept_ref, slab_ref, state_in_ref, beside_ref, out_ref, own_ref = refs[:6]
-    weight_ref, cross_ref, field_ref, state_ref, near_ref, sems = refs[6:]
-    fetches = []
-    for b in range(BINS):
-        fetches.append(pltpu.make_async_copy(kept_ref.at[b], near_ref.at[b], sems.at[b]))
-        fetches[-1].start()
+    pixels_refs, refs = refs[:BINS], refs[BINS:]
+    slab_ref, state_in_ref, beside_ref, out_ref, own_ref = refs[:5]
+    weight_ref, cross_ref, field_ref, state_ref = refs[5:]
     tile = lax.axis_index("tile")
     core = lax.axis_index("frame")
     beside = neighbour_tile(tile, core, tiles)
@@ -378,7 +373,7 @@
                 line = repeated[b * COLOURS + g + i : b * COLOURS + g + i + 1]
                 pair.append(jnp.where(same_row, line, 0.0))
             weight_ref[b, 8 * g : 8 * g + 16, :] = jnp.concatenate(pair, axis=0).astype(bf16)
-        field_ref[b] = dot(weight_ref[b, :, 512:], far_refs[b][...])
+        field_ref[b] = dot(weight_ref[b], pixels_refs[b][...])
     for b in range(BINS):
         rows = slice(b * COLOURS, (b + 1) * COLOURS)
         now = both[rows]
@@ -386,10 +381,6 @@
         for g in range(COLOURS):
             column = jnp.broadcast_to(cross[:, g : g + 1], (COLOURS, EDGE))
             cross_ref[(b * COLOURS + g) * 16 : (b * COLOURS + g) * 16 + 16, :] = column
-    for b in range(BINS):
-        fetches[b].wait()
-        field_ref[b] = field_ref[b] + dot(weight_ref[b, :, :512], near_ref[b])
-
     floor = floor_share * FRAMES
 
     def update(step, carry):
@@ -429,7 +420,7 @@
 
 def patch_kernel(
     rows_ref, cols_ref, colour_ref, state_ref, own_ref, recv_ref, sib_own_ref, sib_recv_ref,
-    out_ref, traces_ref, framed_ref,
+    out_ref, traces_ref, framed_ref, made_ref, sems,
 ):
     tile = lax.axis_index("tile")
     own = state_ref[GROUP:, :]
@@ -445,6 +436,7 @@
     base = jnp.where(block == 0, home, jnp.where(block == 1, edge, jnp.where(block == 2, far_home, far_edge)))
     row_at = base + line % HALF - HALF - iota((PATCH, EDGE), 0)
     col_at = iota((EDGE, PATCH), 0) - iota((EDGE, PATCH), 1)
+    writes = []
     for s in range(SLOTS):
         at = (s // LAYERS) * COLOURS + colour_ref[tile * SLOTS + s]
         traces_ref[s : s + 1, :] = framed_ref[pl.ds(at, 1), :]
@@ -452,7 +444,15 @@
         col_pick = jnp.where(col_at == cols_ref[s], 1.0, 0.0).astype(bf16)
         whole = jnp.concatenate([own_ref[s], recv_ref[s], sib_own_ref[s], sib_recv_ref[s]], axis=0)
         lifted = dot(row_pick, whole).astype(bf16)
-        out_ref[s] = dot(lifted, col_pick).astype(bf16)
+        made_ref[s] = dot(lifted, col_pick).astype(bf16)
+        if s % LAYERS == LAYERS - 1:
+            part = slice(s - LAYERS + 1, s + 1)
+            writes.append(
+                pltpu.make_async_copy(made_ref.at[part], out_ref.at[part], sems.at[s // LAYERS])
+            )
+            writes[-1].start()
+    for write in writes:
+        write.wait()
 
 
 def shape(dims, dtype=f32):
@@ -517,60 +517,56 @@
     )(in_hbm(neuron_live), in_hbm(traces), in_hbm(movie_block))
     begin_far = chip_swap(begin)
 
-    slab, message, kept, *far_pixels = call(
+    slab, message, *pixels = call(
         functools.partial(partial_kernel, tiles),
         [smem] + [vmem] * 6,
-        [
-            shape((GROUP, HALF, EDGE), bf16), shape((2 * GROUP + COLOURS, FRAMES)),
-            pltpu.HBM((BINS, 512, 512), bf16),
-        ]
-        + [shape((512, 512), bf16)] * BINS,
+        [shape((GROUP, HALF, EDGE), bf16), shape((2 * GROUP + COLOURS, FRAMES))]
+        + [shape((1024, 512), bf16)] * BINS,
         "partial_sums",
         12,
-        [pltpu.VMEM((BINS, 512, 512), bf16), pltpu.SemaphoreType.DMA((BINS,))],
-        [vmem, vmem, hbm] + [vmem] * BINS,
     )(neuron_colour, movie_strip, movie_far, piece_own, piece_recv, begin, begin_far)
 
     packed_shape, side_shape = shape((PACKED, FRAMES)), shape((SIDE, FRAMES))
     state_shape = shape((2 * GROUP, FRAMES))
     (packed,) = call(pack_kernel, [vmem] * 2, [packed_shape], "pack", 2)(message, chip_swap(message))
     pair = pair_swap(packed)
+    counter = shape((1, 1), jnp.int32)
     phases, repeat, phase_count = call(
         table_kernel,
         [smem, vmem],
-        [shape((GROUP, FRAMES), jnp.int32), shape((FRAMES, 1024), bf16), shape((1,), jnp.int32)],
+        [shape((GROUP, FRAMES), jnp.int32), shape((FRAMES, 1024), bf16), counter],
         "tables",
         2,
         [pltpu.SMEM((GROUP,), jnp.int32)],
-        [vmem, vmem, smem],
     )(neuron_colour, packed)
     (onward,) = call(
         functools.partial(forward_kernel, tiles), [vmem] * 3, [packed_shape], "forward", 2
     )(packed, pair, phases)
     beyond = lax.ppermute(onward, ("tile", "frame"), far_pairs)
     (side,) = call(side_kernel, [vmem] * 3, [side_shape], "side", 2)(packed, pair, beyond)
-    state, change, gram, before, beside = call(
+    state, change, gram, before, beside, left = call(
         window_kernel,
-        [vmem] * 4,
-        [state_shape, group, shape((2 * COLOURS, FRAMES)), group, group],
+        [vmem] * 5,
+        [state_shape, group, shape((2 * COLOURS, FRAMES)), group, group, counter],
         "window",
         8,
-    )(phases, packed, side, chip_swap(side))
+    )(phase_count, phases, packed, side, chip_swap(side))
 
     def advance(carry):
-        step, state, before, change, _ = carry
+        left, state, before, change, _ = carry
         delta = pair_swap(change)
-        state, change, before = call(
-            next_phase_kernel, [smem] + [vmem] * 6, [state_shape, group, group], "next_phase", 4
-        )(step.reshape(1), phases, gram, state, before, delta, chip_swap(delta))
-        return step + 1, state, before, change, before + pair_swap(change)
-
-    carry = (jnp.int32(2), state, before, change, beside)
-    _, state, _, _, beside = lax.while_loop(lambda c: c[0] < phase_count[0], advance, carry)
+        state, change, before, left = call(
+            next_phase_kernel, [vmem] * 8, [state_shape, group, group, counter], "next_phase", 4
+        )(left, phase_count, phases, gram, state, before, delta, chip_swap(delta))
+        (beside,) = call(add_kernel, [vmem] * 2, [group], "add", 2)(before, pair_swap(change))
+        return left, state, before, change, beside
+
+    carry = (left, state, before, change, beside)
+    _, state, _, _, beside = lax.while_loop(lambda c: (c[0] > 0).reshape(()), advance, carry)
 
     final_out, final_own = call(
         functools.partial(spatial_kernel, tiles),
-        [smem] + [vmem] * 5 + [hbm] + [vmem] * 3,
+        [smem] + [vmem] * 8,
         [piece, piece],
         "spatial",
         10,
@@ -579,10 +575,8 @@
             pltpu.VMEM((GROUP * COLOURS, EDGE), f32),
             pltpu.VMEM((BINS, 128, 512), f32),
             pltpu.VMEM((GROUP, HALF, EDGE), bf16),
-            pltpu.VMEM((BINS, 512, 512), bf16),
-            pltpu.SemaphoreType.DMA((BINS,)),
         ],
-    )(neuron_colour, repeat, *far_pixels, in_hbm(kept), slab, state, beside)
+    )(neuron_colour, repeat, *pixels, slab, state, beside)
 
     far_own = chip_swap(final_own)
     final_recv = pair_swap(final_out)
@@ -593,7 +587,12 @@
         [shape((SLOTS, PATCH, PATCH), bf16), shape((SLOTS, 64))],
         "patches",
         8,
-        [pltpu.VMEM((GROUP, 64), f32)],
+        [
+            pltpu.VMEM((GROUP, 64), f32),
+            pltpu.VMEM((SLOTS, PATCH, PATCH), bf16),
+            pltpu.SemaphoreType.DMA((BINS,)),
+        ],
+        [hbm, vmem],
     )(patch_rows, patch_cols, neuron_colour, state, final_own, final_recv, far_own, far_recv)
     return (new_traces, new_patches)
 

time: 67.5 us -> 66.6 us (0.987)
  Pallas kernels: 18.8 us -> 18 us
    pallas_call x1, Pallas kernels: 3.92 us -> 2.72 us  [on_device(): call(functools.partial(partial_kernel, tiles), [smem] + [vmem] * 6, [shap...]
where the time goes in v1:
time: 66.6 us; the launch traced here: 65.9 us
  starting transfers between devices  28.6 us (43%)
  Pallas kernels  18 us (27%)
  waiting for transfers between devices  17.8 us (27%)
  between operations  0.78 us (1%)
  loops' own time  0.7 us (1%)
    ppermute x3, starting transfers between devices, pair_swap(): return lax.ppermute(value, ('tile', 'frame'), swap_pairs)  26.3 us
    ppermute x1, waiting for transfers between devices, on_device(): beyond = lax.ppermute(onward, ('tile', 'frame'), far_pairs)  7.19 us
    ppermute x6, waiting for transfers between devices, chip_swap(): return lax.ppermute(value, 'frame', [(0, 1), (1, 0)])  5.38 us
    ppermute x3, waiting for transfers between devices, pair_swap(): return lax.ppermute(value, ('tile', 'frame'), swap_pairs)  5.25 us
    pallas_call x1, Pallas kernels, on_device(): call(functools.partial(spatial_kernel, tiles), [smem] + [vmem] * 8, [piec...  3.53 us
    pallas_call x1, Pallas kernels, on_device(): call(patch_kernel, [smem] * 3 + [vmem] * 5, [shape((SLOTS, PATCH, PATCH),...  2.89 us
    pallas_call x1, Pallas kernels, on_device(): call(functools.partial(partial_kernel, tiles), [smem] + [vmem] * 6, [shap...  2.72 us
    pallas_call x1, Pallas kernels, on_device(): call(window_kernel, [vmem] * 5, [state_shape, group, shape((2 * COLOURS,...  2.69 us
  transfers between devices with their start and end apart: 10, of which 8 were waited for; matrix products, arithmetic and copies ran while one was open for 0% of the time, Pallas kernels for 9%

profile of v1, /device:TPU:6, one launch (start us, length us, event | category | flops | bytes accessed | tf_op | source)
XLA Modules:
  0.0 65.9 jit_solution(14254650376384611521)
XLA Ops:
  0.6 0.0 copy-start
  0.6 0.1 collective-permute-start.3
  0.7 2.2 %slabs.1 = (bf16[32,32,128]{2,1,0:T(8,128)(2,1)S(1)}, bf16[32,32,128]{2,1,0:T(8,128)(2,1)S(1)}) custom-call(s32[32]{0:T(128)} %rows_ref.3, s32[32]{0:T(128)} %cols_ref.3, s32[32]{0:T(128)} %live_ref.3, bf16[32,64,64]{2,1,0:T(8,128)(2,1)} %patches_ref.1), custom_call_target="tpu_custom_call" | custom-call | tf_op jit(solution)/shard_map/slabs/pallas_call | solution.py:497
  2.9 10.6 %collective-permute-start.4 = (bf16[32,32,128]{2,1,0:T(8,128)(2,1)S(1)}, bf16[32,32,128]{2,1,0:T(8,128)(2,1)S(1)}, u32[]{:S(2)}, u32[]{:S(2)}) collective-permute-start(bf16[32,32,128]{2,1,0:T(8,128)(2,1)S(1)} %get-tuple-element.73), channel_id=1, source_target_pairs={{1,2},{2,1},{3,4},{4,3},{5,6},{6,5},{7,8},{8,7},{9,10},{10,9},{11,... | collective-permute-start | bytes 786440 | tf_op jit(solution)/shard_map/ppermute | solution.py:481
  13.5 2.3 %fetch.1 = (f32[32,64]{1,0:T(8,128)S(1)}, bf16[64,32,512]{2,1,0:T(8,128)(2,1)S(1)}) custom-call(s32[32]{0:T(128)} %live_ref.3, f32[32,64]{1,0:T(8,128)} %traces_ref.1, bf16[64,64,512]{2,1,0:T(8,128)(2,1)} %movie_ref.1), custom_call_target="tpu_custom_call" | custom-call | tf_op jit(solution)/shard_map/fetch/pallas_call | solution.py:510
  15.9 0.1 collective-permute-start.5
  16.0 1.2 %collective-permute-done.5.far_ref = f32[32,64]{1,0:T(8,128)S(1)} collective-permute-done((f32[32,64]{1,0:T(8,128)S(1)}, f32[32,64]{1,0:T(8,128)S(1)}, u32[]{:S(2)}, u32[]{:S(2)}) %collective-permute-start.5) | collective-permute-done | bytes 8224 | tf_op jit(solution)/shard_map/ppermute | solution.py:488
  17.1 0.5 collective-permute-done.4.recv_ref
  17.6 0.0 collective-permute-done.3.other_ref
  17.6 0.0 copy-done
  17.6 2.7 %partial_sums.1 = (bf16[64,32,128]{2,1,0:T(8,128)(2,1)S(1)}, f32[144,128]{1,0:T(8,128)S(1)}, bf16[1024,512]{1,0:T(8,128)(2,1)S(1)}, bf16[1024,512]{1,0:T(8,128)(...) custom-call(s32[4096]{0:T(1024)S(1)} %copy-done, ...), custom_call_target="tpu_custom_call" | custom-call | tf_op jit(solution)/shard_map/partial_sums/pallas_call | solution.py:520
  20.3 0.0 collective-permute-start.6
  20.3 1.3 %collective-permute-done.6.far_ref = f32[144,128]{1,0:T(8,128)S(1)} collective-permute-done((f32[144,128]{1,0:T(8,128)S(1)}, f32[144,128]{1,0:T(8,128)S(1)}, u32[]{:S(2)}, u32[]{:S(2)}) %collective-permute-start.6) | collective-permute-done | bytes 73760 | tf_op jit(solution)/shard_map/ppermute | solution.py:488
  21.6 7.9 %collective-permute-start.7 = (f32[224,128]{1,0:T(8,128)S(1)}, f32[224,128]{1,0:T(8,128)S(1)}, u32[]{:S(2)}, u32[]{:S(2)}) collective-permute-start(f32[224,128]{1,0:T(8,128)S(1)} %pack.1.anchor_ref.pack_ref), channel_id=1, source_target_pairs={{1,2},{2,1},{3,4},{4,3},{5,6},{6,5},{7,8},{8,7},{9,10},{10,9},{11,... | collective-permute-start | bytes 344072 | tf_op jit(solution)/shard_map/ppermute | solution.py:481
  29.5 1.6 %tables.1 = (s32[64,128]{1,0:T(8,128)S(1)}, bf16[128,1024]{1,0:T(8,128)(2,1)S(1)}, s32[1,1]{1,0:T(1,128)}) custom-call(s32[4096]{0:T(1024)S(1)} %copy-done, f32[224,128]{1,0:T(8,128)S(1)} %pack.1.anchor_ref.pack_ref), custom_call_target="tpu_custom_call" | custom-call | tf_op jit(solution)/shard_map/tables/pallas_call | solution.py:534
  31.1 0.9 %collective-permute-done.7.pair_ref = f32[224,128]{1,0:T(8,128)S(1)} collective-permute-done((f32[224,128]{1,0:T(8,128)S(1)}, f32[224,128]{1,0:T(8,128)S(1)}, u32[]{:S(2)}, u32[]{:S(2)}) %collective-permute-start.7) | collective-permute-done | bytes 114720 | tf_op jit(solution)/shard_map/ppermute | solution.py:481
  32.0 1.9 %collective-permute-start.8 = (f32[224,128]{1,0:T(8,128)S(1)}, f32[224,128]{1,0:T(8,128)S(1)}, u32[]{:S(2)}, u32[]{:S(2)}) collective-permute-start(f32[224,128]{1,0:T(8,128)S(1)} %forward.1), channel_id=1, source_target_pairs={{255,251},{0,4},{1,6},{6,1},{3,8},{8,3},{5,10},{10,5},{7,12},{12,7... | collective-permute-start | bytes 344072 | tf_op jit(solution)/shard_map/ppermute | solution.py:545
  33.9 7.2 %collective-permute-done.8.beyond_ref = f32[224,128]{1,0:T(8,128)S(1)} collective-permute-done((f32[224,128]{1,0:T(8,128)S(1)}, f32[224,128]{1,0:T(8,128)S(1)}, u32[]{:S(2)}, u32[]{:S(2)}) %collective-permute-start.8) | collective-permute-done | bytes 114720 | tf_op jit(solution)/shard_map/ppermute | solution.py:545
  41.1 0.0 copy-start.1
  41.1 0.0 copy-start.2
  41.1 0.1 collective-permute-start.9
  41.2 1.4 %collective-permute-done.9.there_ref = f32[368,128]{1,0:T(8,128)S(1)} collective-permute-done((f32[368,128]{1,0:T(8,128)S(1)}, f32[368,128]{1,0:T(8,128)S(1)}, u32[]{:S(2)}, u32[]{:S(2)}) %collective-permute-start.9) | collective-permute-done | bytes 188448 | tf_op jit(solution)/shard_map/ppermute | solution.py:488
  42.6 2.7 %window.1 = (f32[128,128]{1,0:T(8,128)S(1)}, f32[64,128]{1,0:T(8,128)S(1)}, f32[32,128]{1,0:T(8,128)S(1)}, f32[64,128]{1,0:T(8,128)S(1)}, f32[64,128]{1,0:T(8,128)}, /*index=5*/s32[1,1]{1,0:T(1,128)}) custom-call(s32[1,1]{1,0:T(1,128)} %get-tuple-element.125.count_ref, s32[64,128]{1,0:T(8,128)S(1)} %get-tuple-element.126.anchor_ref.phase_ref, ...), custom_call_target="tpu_custom_call" | custom-call | tf_op jit(solution)/shard_map/window/pallas_call | solution.py:547
  45.3 0.7 %while.15 = (s32[1,1]{1,0:T(1,128)}, f32[128,128]{1,0:T(8,128)S(1)}, f32[64,128]{1,0:T(8,128)S(1)}, f32[64,128]{1,0:T(8,128)S(1)}, f32[64,128]{1,0:T(8,128)}, /*...) while((s32[1,1]{1,0:T(1,128)}, f32[128,128]{1,0:T(8,128)S(1)}, f32[64,128]{1,0:T(8,128)S(1)}, ...), condition=%region_1.0_spmd, body=%region_0.0_spmd | while | flops 1 | bytes 590025 | solution.py:565
  46.0 3.5 %spatial.1 = (bf16[32,32,128]{2,1,0:T(8,128)(2,1)S(1)}, bf16[32,32,128]{2,1,0:T(8,128)(2,1)S(1)}) custom-call(s32[4096]{0:T(1024)S(1)} %copy-done, bf16[128,1024]{1,0:T(8,128)(2,1)S(1)} %get-tuple-element.85.repeat_ref, bf16[1024,512]{1,0:T(8,128)(2,1)S(1)} %get-tuple-element.86.refs_0_, bf16[1024,512]{1,0:T(8,128)(2,1)S(1)} %get-tuple-element.87.refs_1_, ...), custom_call_target="tpu_custom_call" | custom-call | tf_op jit(solution)/shard_map/spatial/pallas_call | solution.py:567
  49.6 7.9 %collective-permute-start.10 = (bf16[32,32,128]{2,1,0:T(8,128)(2,1)S(1)}, bf16[32,32,128]{2,1,0:T(8,128)(2,1)S(1)}, u32[]{:S(2)}, u32[]{:S(2)}) collective-permute-start(bf16[32,32,128]{2,1,0:T(8,128)(2,1)S(1)} %get-tuple-element.93), channel_id=1, source_target_pairs={{1,2},{2,1},{3,4},{4,3},{5,6},{6,5},{7,8},{8,7},{9,10},{10,9},{11,... | collective-permute-start | bytes 786440 | tf_op jit(solution)/shard_map/ppermute | solution.py:481
  57.4 0.1 collective-permute-start.11
  57.5 3.9 %collective-permute-done.10.recv_ref = bf16[32,32,128]{2,1,0:T(8,128)(2,1)S(1)} collective-permute-done((bf16[32,32,128]{2,1,0:T(8,128)(2,1)S(1)}, bf16[32,32,128]{2,1,0:T(8,128)(2,1)S(1)}, u32[]{:S(2)}, u32[]{:S(2)}) %collective-permute-start.10) | collective-permute-done | bytes 262176 | tf_op jit(solution)/shard_map/ppermute | solution.py:481
  61.5 0.0 collective-permute-start.12
  61.5 0.0 collective-permute-done.11.sib_own_ref
  61.5 1.5 %collective-permute-done.12.sib_recv_ref = bf16[32,32,128]{2,1,0:T(8,128)(2,1)S(1)} collective-permute-done((bf16[32,32,128]{2,1,0:T(8,128)(2,1)S(1)}, bf16[32,32,128]{2,1,0:T(8,128)(2,1)S(1)}, u32[]{:S(2)}, u32[]{:S(2)}) %collective-permute-start.12) | collective-permute-done | bytes 262176 | tf_op jit(solution)/shard_map/ppermute | solution.py:488
  63.0 0.0 copy-done.1
  63.0 0.0 copy-done.2
  63.0 2.9 %patches.1 = (bf16[32,64,64]{2,1,0:T(8,128)(2,1)}, f32[32,64]{1,0:T(8,128)}) custom-call(s32[32]{0:T(128)S(1)} %copy-done.1, s32[32]{0:T(128)S(1)} %copy-done.2, s32[4096]{0:T(1024)S(1)} %copy-done, f32[128,128]{1,0:T(8,128)S(1)} %get-tuple-element.84.refs_5_.state_ref, bf16[32,32,128]{2,1,0:T(8,128)(2,1)S(1)} %get-tuple-element.92.own_ref, ...), custom_call_target="tpu_custom_call" | custom-call | tf_op jit(solution)/shard_map/patches/pallas_call | solution.py:584
  (3 shorter events, 0.0 us)
Async XLA Ops:
  0.6 17.0 %copy-start = (s32[4096]{0:T(1024)S(1)}, s32[4096]{0:T(1024)}, u32[]{:S(2)}) copy-start(s32[4096]{0:T(1024)} %colour_ref.7) | copy-start | bytes 49156
  0.6 17.0 %collective-permute-start.3 = (bf16[64,64,512]{2,1,0:T(8,128)(2,1)}, bf16[64,64,512]{2,1,0:T(8,128)(2,1)S(1)}, u32[]{:S(2)}, u32[]{:S(2)}) collective-permute-start(bf16[64,64,512]{2,1,0:T(8,128)(2,1)} %movie_ref.1), channel_id=1, source_target_pairs={{0,1},{1,0},{2,3},{3,2},{4,5},{5,4},{6,7},{7,6},{8,9},{9,8},{10,11... | collective-permute-start | bytes 12582920 | tf_op jit(solution)/shard_map/ppermute | solution.py:488
  2.9 14.7 %collective-permute-start.4 = (bf16[32,32,128]{2,1,0:T(8,128)(2,1)S(1)}, bf16[32,32,128]{2,1,0:T(8,128)(2,1)S(1)}, u32[]{:S(2)}, u32[]{:S(2)}) collective-permute-start(bf16[32,32,128]{2,1,0:T(8,128)(2,1)S(1)} %get-tuple-element.73), channel_id=1, source_target_pairs={{1,2},{2,1},{3,4},{4,3},{5,6},{6,5},{7,8},{8,7},{9,10},{10,9},{11,... | collective-permute-start | bytes 786440 | tf_op jit(solution)/shard_map/ppermute | solution.py:481
  15.9 1.3 %collective-permute-start.5 = (f32[32,64]{1,0:T(8,128)S(1)}, f32[32,64]{1,0:T(8,128)S(1)}, u32[]{:S(2)}, u32[]{:S(2)}) collective-permute-start(f32[32,64]{1,0:T(8,128)S(1)} %get-tuple-element.74.near_ref), channel_id=1, source_target_pairs={{0,1},{1,0},{2,3},{3,2},{4,5},{5,4},{6,7},{7,6},{8,9},{9,8},{10,11... | collective-permute-start | bytes 24584 | tf_op jit(solution)/shard_map/ppermute | solution.py:488
  20.3 1.3 %collective-permute-start.6 = (f32[144,128]{1,0:T(8,128)S(1)}, f32[144,128]{1,0:T(8,128)S(1)}, u32[]{:S(2)}, u32[]{:S(2)}) collective-permute-start(f32[144,128]{1,0:T(8,128)S(1)} %get-tuple-element.75.mine_ref), channel_id=1, source_target_pairs={{0,1},{1,0},{2,3},{3,2},{4,5},{5,4},{6,7},{7,6},{8,9},{9,8},{10,11... | collective-permute-start | bytes 221192 | tf_op jit(solution)/shard_map/ppermute | solution.py:488
  21.6 10.3 %collective-permute-start.7 = (f32[224,128]{1,0:T(8,128)S(1)}, f32[224,128]{1,0:T(8,128)S(1)}, u32[]{:S(2)}, u32[]{:S(2)}) collective-permute-start(f32[224,128]{1,0:T(8,128)S(1)} %pack.1.anchor_ref.pack_ref), channel_id=1, source_target_pairs={{1,2},{2,1},{3,4},{4,3},{5,6},{6,5},{7,8},{8,7},{9,10},{10,9},{11,... | collective-permute-start | bytes 344072 | tf_op jit(solution)/shard_map/ppermute | solution.py:481
  32.0 9.1 %collective-permute-start.8 = (f32[224,128]{1,0:T(8,128)S(1)}, f32[224,128]{1,0:T(8,128)S(1)}, u32[]{:S(2)}, u32[]{:S(2)}) collective-permute-start(f32[224,128]{1,0:T(8,128)S(1)} %forward.1), channel_id=1, source_target_pairs={{255,251},{0,4},{1,6},{6,1},{3,8},{8,3},{5,10},{10,5},{7,12},{12,7... | collective-permute-start | bytes 344072 | tf_op jit(solution)/shard_map/ppermute | solution.py:545
  41.1 21.9 %copy-start.1 = (s32[32]{0:T(128)S(1)}, s32[32]{0:T(128)}, u32[]{:S(2)}) copy-start(s32[32]{0:T(128)} %rows_ref.3) | copy-start | bytes 388
  41.1 21.9 %copy-start.2 = (s32[32]{0:T(128)S(1)}, s32[32]{0:T(128)}, u32[]{:S(2)}) copy-start(s32[32]{0:T(128)} %cols_ref.3) | copy-start | bytes 388
  41.1 1.5 %collective-permute-start.9 = (f32[368,128]{1,0:T(8,128)S(1)}, f32[368,128]{1,0:T(8,128)S(1)}, u32[]{:S(2)}, u32[]{:S(2)}) collective-permute-start(f32[368,128]{1,0:T(8,128)S(1)} %side.1.here_ref), channel_id=1, source_target_pairs={{0,1},{1,0},{2,3},{3,2},{4,5},{5,4},{6,7},{7,6},{8,9},{9,8},{10,11... | collective-permute-start | bytes 565256 | tf_op jit(solution)/shard_map/ppermute | solution.py:488
  49.6 11.9 %collective-permute-start.10 = (bf16[32,32,128]{2,1,0:T(8,128)(2,1)S(1)}, bf16[32,32,128]{2,1,0:T(8,128)(2,1)S(1)}, u32[]{:S(2)}, u32[]{:S(2)}) collective-permute-start(bf16[32,32,128]{2,1,0:T(8,128)(2,1)S(1)} %get-tuple-element.93), channel_id=1, source_target_pairs={{1,2},{2,1},{3,4},{4,3},{5,6},{6,5},{7,8},{8,7},{9,10},{10,9},{11,... | collective-permute-start | bytes 786440 | tf_op jit(solution)/shard_map/ppermute | solution.py:481
  57.4 4.0 %collective-permute-start.11 = (bf16[32,32,128]{2,1,0:T(8,128)(2,1)S(1)}, bf16[32,32,128]{2,1,0:T(8,128)(2,1)S(1)}, u32[]{:S(2)}, u32[]{:S(2)}) collective-permute-start(bf16[32,32,128]{2,1,0:T(8,128)(2,1)S(1)} %get-tuple-element.92.own_ref), channel_id=1, source_target_pairs={{0,1},{1,0},{2,3},{3,2},{4,5},{5,4},{6,7},{7,6},{8,9},{9,8},{10,11... | collective-permute-start | bytes 786440 | tf_op jit(solution)/shard_map/ppermute | solution.py:488
  61.5 1.5 %collective-permute-start.12 = (bf16[32,32,128]{2,1,0:T(8,128)(2,1)S(1)}, bf16[32,32,128]{2,1,0:T(8,128)(2,1)S(1)}, u32[]{:S(2)}, u32[]{:S(2)}) collective-permute-start(bf16[32,32,128]{2,1,0:T(8,128)(2,1)S(1)} %collective-permute-done.10.recv_ref), channel_id=1, source_target_pairs={{0,1},{1,0},{2,3},{3,2},{4,5},{5,4},{6,7},{7,6},{8,9},{9,8},{10,11... | collective-permute-start | bytes 786440 | tf_op jit(solution)/shard_map/ppermute | solution.py:488

commit v2 on v1

--- a/solution.py
+++ b/solution.py
@@ -75,16 +75,20 @@
         own_ref[s] = jnp.where(core == 0, lower, upper)
 
 
-def fetch_kernel(live_ref, traces_ref, movie_ref, begin_ref, strip_ref, sems):
+def fetch_kernel(
+    live_ref, traces_ref, far_ref, movie_ref, begin_ref, begin_far_ref, strip_ref, sems
+):
     first = pl.multiple_of(HALF * lax.axis_index("frame"), HALF)
     fetches = fetch_rows(movie_ref, strip_ref, first, sems)
     for s in range(SLOTS):
-        begin_ref[s : s + 1, :] = traces_ref[s : s + 1, :] * live_ref[s].astype(f32)
+        alive = live_ref[s].astype(f32)
+        begin_ref[s : s + 1, :] = traces_ref[s : s + 1, :] * alive
+        begin_far_ref[s : s + 1, :] = far_ref[s : s + 1, :] * alive
     for fetch in fetches:
         fetch.wait()
 
 
-def table_kernel(colour_ref, anchor_ref, phase_ref, repeat_ref, count_ref, owner_ref):
+def table_kernel(colour_ref, anchor_ref, phase_ref, repeat_ref, count_ref, left_ref, owner_ref):
     tile = lax.axis_index("tile")
     for i in range(GROUP):
         owner_ref[i] = 0
@@ -102,6 +106,7 @@
             phase_ref[i : i + 1, :] = jnp.full((1, FRAMES), value, jnp.int32)
         most = jnp.maximum(most, phase + 1)
     count_ref[...] = jnp.full((1, 1), most, jnp.int32)
+    left_ref[...] = jnp.full((1, 1), most - 2, jnp.int32)
     position = (iota((FRAMES, 1024), 1) // 8 + 64 * lax.axis_index("frame")) % FRAMES
     repeat_ref[...] = jnp.where(position == iota((FRAMES, 1024), 0), 1.0, 0.0).astype(bf16)
 
@@ -292,10 +297,8 @@
 
 
 def window_kernel(
-    count_ref, phase_ref, pack_ref, here_ref, there_ref, state_ref, change_ref, gram_ref, before_ref,
-    beside_ref, left_ref,
+    phase_ref, pack_ref, here_ref, there_ref, state_ref, change_ref, gram_ref, before_ref, beside_ref
 ):
-    left_ref[...] = count_ref[...] - 2
     phase = phase_ref[...]
     own = phase < 100
     start = pack_ref[all_traces, :]
@@ -419,13 +422,8 @@
 
 
 def patch_kernel(
-    rows_ref, cols_ref, colour_ref, state_ref, own_ref, recv_ref, sib_own_ref, sib_recv_ref,
-    out_ref, traces_ref, framed_ref, made_ref, sems,
+    rows_ref, cols_ref, own_ref, recv_ref, sib_own_ref, sib_recv_ref, out_ref
 ):
-    tile = lax.axis_index("tile")
-    own = state_ref[GROUP:, :]
-    rolled = jnp.concatenate([own[:, 64:], own[:, :64]], axis=1)
-    framed_ref[...] = jnp.where(lax.axis_index("frame") == 0, own, rolled)[:, :64]
     core = lax.axis_index("frame")
     line = iota((PATCH, EDGE), 1)
     block = line // HALF
@@ -436,23 +434,23 @@
     base = jnp.where(block == 0, home, jnp.where(block == 1, edge, jnp.where(block == 2, far_home, far_edge)))
     row_at = base + line % HALF - HALF - iota((PATCH, EDGE), 0)
     col_at = iota((EDGE, PATCH), 0) - iota((EDGE, PATCH), 1)
-    writes = []
-    for s in range(SLOTS):
-        at = (s // LAYERS) * COLOURS + colour_ref[tile * SLOTS + s]
-        traces_ref[s : s + 1, :] = framed_ref[pl.ds(at, 1), :]
+    for s in range(SLOTS):
         row_pick = jnp.where(row_at == rows_ref[s], 1.0, 0.0).astype(bf16)
         col_pick = jnp.where(col_at == cols_ref[s], 1.0, 0.0).astype(bf16)
         whole = jnp.concatenate([own_ref[s], recv_ref[s], sib_own_ref[s], sib_recv_ref[s]], axis=0)
         lifted = dot(row_pick, whole).astype(bf16)
-        made_ref[s] = dot(lifted, col_pick).astype(bf16)
-        if s % LAYERS == LAYERS - 1:
-            part = slice(s - LAYERS + 1, s + 1)
-            writes.append(
-                pltpu.make_async_copy(made_ref.at[part], out_ref.at[part], sems.at[s // LAYERS])
-            )
-            writes[-1].start()
-    for write in writes:
-        write.wait()
+        out_ref[s] = dot(lifted, col_pick).astype(bf16)
+
+
+def traces_kernel(colour_ref, state_ref, own_ref, traces_ref, own_out_ref, framed_ref):
+    tile = lax.axis_index("tile")
+    own = state_ref[GROUP:, :]
+    rolled = jnp.concatenate([own[:, 64:], own[:, :64]], axis=1)
+    framed_ref[...] = jnp.where(lax.axis_index("frame") == 0, own, rolled)[:, :64]
+    for s in range(SLOTS):
+        at = (s // LAYERS) * COLOURS + colour_ref[tile * SLOTS + s]
+        traces_ref[s : s + 1, :] = framed_ref[pl.ds(at, 1), :]
+    own_out_ref[...] = own_ref[...]
 
 
 def shape(dims, dtype=f32):
@@ -494,6 +492,7 @@
     group = shape((GROUP, FRAMES))
     hbm = pl.BlockSpec(memory_space=pltpu.HBM)
     movie_far = chip_swap(movie_block)
+    traces_far = chip_swap(traces)
     piece_out, piece_own = call(
         slab_kernel,
         [smem, smem, smem, hbm],
@@ -507,15 +506,14 @@
         ],
     )(in_hbm(patch_rows), in_hbm(patch_cols), in_hbm(neuron_live), in_hbm(patches))
     piece_recv = pair_swap(piece_out)
-    begin, movie_strip = call(
+    begin, begin_far, movie_strip = call(
         fetch_kernel,
-        [smem, vmem, hbm],
-        [shape((SLOTS, 64)), shape((64, HALF, 512), bf16)],
+        [smem, vmem, vmem, hbm],
+        [shape((SLOTS, 64)), shape((SLOTS, 64)), shape((64, HALF, 512), bf16)],
         "fetch",
         4,
         [pltpu.SemaphoreType.DMA((8,))],
-    )(in_hbm(neuron_live), in_hbm(traces), in_hbm(movie_block))
-    begin_far = chip_swap(begin)
+    )(in_hbm(neuron_live), in_hbm(traces), traces_far, in_hbm(movie_block))
 
     slab, message, *pixels = call(
         functools.partial(partial_kernel, tiles),
@@ -531,10 +529,11 @@
     (packed,) = call(pack_kernel, [vmem] * 2, [packed_shape], "pack", 2)(message, chip_swap(message))
     pair = pair_swap(packed)
     counter = shape((1, 1), jnp.int32)
-    phases, repeat, phase_count = call(
+    phases, repeat, phase_count, left = call(
         table_kernel,
         [smem, vmem],
-        [shape((GROUP, FRAMES), jnp.int32), shape((FRAMES, 1024), bf16), counter],
+        [shape((GROUP, FRAMES), jnp.int32), shape((FRAMES, 1024), bf16)]
+        + [counter] * 2,
         "tables",
         2,
         [pltpu.SMEM((GROUP,), jnp.int32)],
@@ -544,13 +543,13 @@
     )(packed, pair, phases)
     beyond = lax.ppermute(onward, ("tile", "frame"), far_pairs)
     (side,) = call(side_kernel, [vmem] * 3, [side_shape], "side", 2)(packed, pair, beyond)
-    state, change, gram, before, beside, left = call(
+    state, change, gram, before, beside = call(
         window_kernel,
-        [vmem] * 5,
-        [state_shape, group, shape((2 * COLOURS, FRAMES)), group, group, counter],
+        [vmem] * 4,
+        [state_shape, group, shape((2 * COLOURS, FRAMES)), group, group],
         "window",
         8,
-    )(phase_count, phases, packed, side, chip_swap(side))
+    )(phases, packed, side, chip_swap(side))
 
     def advance(carry):
         left, state, before, change, _ = carry
@@ -578,22 +577,20 @@
         ],
     )(neuron_colour, repeat, *pixels, slab, state, beside)
 
-    far_own = chip_swap(final_own)
+    new_traces, kept_own = call(
+        traces_kernel,
+        [smem, vmem, vmem],
+        [shape((SLOTS, 64)), piece],
+        "traces",
+        2,
+        [pltpu.VMEM((GROUP, 64), f32)],
+    )(neuron_colour, state, final_own)
+    far_own = chip_swap(kept_own)
     final_recv = pair_swap(final_out)
     far_recv = chip_swap(final_recv)
-    new_patches, new_traces = call(
-        patch_kernel,
-        [smem] * 3 + [vmem] * 5,
-        [shape((SLOTS, PATCH, PATCH), bf16), shape((SLOTS, 64))],
-        "patches",
-        8,
-        [
-            pltpu.VMEM((GROUP, 64), f32),
-            pltpu.VMEM((SLOTS, PATCH, PATCH), bf16),
-            pltpu.SemaphoreType.DMA((BINS,)),
-        ],
-        [hbm, vmem],
-    )(patch_rows, patch_cols, neuron_colour, state, final_own, final_recv, far_own, far_recv)
+    (new_patches,) = call(
+        patch_kernel, [smem, smem] + [vmem] * 4, [shape((SLOTS, PATCH, PATCH), bf16)], "patches", 8
+    )(patch_rows, patch_cols, kept_own, final_recv, far_own, far_recv)
     return (new_traces, new_patches)
 
 

time: 66.6 us -> 65.1 us (0.977)
  waiting for transfers between devices: 17.8 us -> 16.4 us
    ppermute x3, waiting for transfers between devices: 5.25 us -> 3.63 us  [pair_swap(): return lax.ppermute(value, ('tile', 'frame'), swap_pairs)]
    pallas_call x3 -> x4, Pallas kernels: 7.89 us -> 7.97 us  [the longest x1 2.3 us: on_device(): call(fetch_kernel, [smem, vmem, vmem, hbm], [shape((SLOTS, 64)), shape((S...]
  transfers between devices with their start and end apart: 10 -> 10, of which waited for: 8 -> 8; matrix products, arithmetic and copies ran while one was open for 0% -> 0% of each run, Pallas kernels for 9% -> 12%
where the time goes in v2:
time: 65.1 us; the launch traced here: 64.5 us
  starting transfers between devices  28.6 us (44%)
  Pallas kernels  18.1 us (28%)
  waiting for transfers between devices  16.4 us (25%)
  between operations  0.76 us (1%)
  loops' own time  0.68 us (1%)
    ppermute x3, starting transfers between devices, pair_swap(): return lax.ppermute(value, ('tile', 'frame'), swap_pairs)  26.3 us
    ppermute x1, waiting for transfers between devices, on_device(): beyond = lax.ppermute(onward, ('tile', 'frame'), far_pairs)  7.19 us
    ppermute x6, waiting for transfers between devices, chip_swap(): return lax.ppermute(value, 'frame', [(0, 1), (1, 0)])  5.58 us
    ppermute x3, waiting for transfers between devices, pair_swap(): return lax.ppermute(value, ('tile', 'frame'), swap_pairs)  3.63 us
    pallas_call x1, Pallas kernels, on_device(): call(functools.partial(spatial_kernel, tiles), [smem] + [vmem] * 8, [piec...  3.53 us
    pallas_call x1, Pallas kernels, on_device(): call(functools.partial(partial_kernel, tiles), [smem] + [vmem] * 6, [shap...  2.72 us
    pallas_call x1, Pallas kernels, on_device(): call(fetch_kernel, [smem, vmem, vmem, hbm], [shape((SLOTS, 64)), shape((S...  2.3 us
    pallas_call x1, Pallas kernels, on_device(): call(slab_kernel, [smem, smem, smem, hbm], [piece, piece], 'slabs', 8, [p...  2.18 us
  transfers between devices with their start and end apart: 10, of which 8 were waited for; matrix products, arithmetic and copies ran while one was open for 0% of the time, Pallas kernels for 12%

profile of v2, /device:TPU:6, one launch (start us, length us, event | category | flops | bytes accessed | tf_op | source)
XLA Modules:
  0.0 64.5 jit_solution(11169685737440163009)
XLA Ops:
  0.6 0.0 copy-start
  0.6 0.1 collective-permute-start.4
  0.7 2.2 %slabs.1 = (bf16[32,32,128]{2,1,0:T(8,128)(2,1)S(1)}, bf16[32,32,128]{2,1,0:T(8,128)(2,1)S(1)}) custom-call(s32[32]{0:T(128)} %rows_ref.3, s32[32]{0:T(128)} %cols_ref.3, s32[32]{0:T(128)} %live_ref.3, bf16[32,64,64]{2,1,0:T(8,128)(2,1)} %patches_ref.1), custom_call_target="tpu_custom_call" | custom-call | tf_op jit(solution)/shard_map/slabs/pallas_call | solution.py:496
  2.9 10.6 %collective-permute-start.5 = (bf16[32,32,128]{2,1,0:T(8,128)(2,1)S(1)}, bf16[32,32,128]{2,1,0:T(8,128)(2,1)S(1)}, u32[]{:S(2)}, u32[]{:S(2)}) collective-permute-start(bf16[32,32,128]{2,1,0:T(8,128)(2,1)S(1)} %get-tuple-element.74), channel_id=1, source_target_pairs={{1,2},{2,1},{3,4},{4,3},{5,6},{6,5},{7,8},{8,7},{9,10},{10,9},{11,... | collective-permute-start | bytes 786440 | tf_op jit(solution)/shard_map/ppermute | solution.py:479
  13.6 0.1 collective-permute-start.3
  13.7 1.4 %collective-permute-done.3.far_ref = f32[32,64]{1,0:T(8,128)S(1)} collective-permute-done((f32[32,64]{1,0:T(8,128)}, f32[32,64]{1,0:T(8,128)S(1)}, u32[]{:S(2)}, u32[]{:S(2)}) %collective-permute-start.3) | collective-permute-done | bytes 8224 | tf_op jit(solution)/shard_map/ppermute | solution.py:486
  15.0 2.3 %fetch.1 = (f32[32,64]{1,0:T(8,128)S(1)}, f32[32,64]{1,0:T(8,128)S(1)}, bf16[64,32,512]{2,1,0:T(8,128)(2,1)S(1)}) custom-call(s32[32]{0:T(128)} %live_ref.3, f32[32,64]{1,0:T(8,128)} %traces_ref.1, f32[32,64]{1,0:T(8,128)S(1)} %collective-permute-done.3.far_ref, bf16[64,64,512]{2,1,0:T(8,128)(2,1)} %movie_ref.1), custom_call_target="tpu_custom_call" | custom-call | tf_op jit(solution)/shard_map/fetch/pallas_call | solution.py:509
  17.3 0.2 collective-permute-done.5.recv_ref
  17.6 0.0 collective-permute-done.4.other_ref
  17.6 0.0 copy-done
  17.6 2.7 %partial_sums.1 = (bf16[64,32,128]{2,1,0:T(8,128)(2,1)S(1)}, f32[144,128]{1,0:T(8,128)S(1)}, bf16[1024,512]{1,0:T(8,128)(2,1)S(1)}, bf16[1024,512]{1,0:T(8,128)(...) custom-call(s32[4096]{0:T(1024)S(1)} %copy-done, ...), custom_call_target="tpu_custom_call" | custom-call | tf_op jit(solution)/shard_map/partial_sums/pallas_call | solution.py:518
  20.3 0.0 collective-permute-start.6
  20.3 1.3 %collective-permute-done.6.far_ref = f32[144,128]{1,0:T(8,128)S(1)} collective-permute-done((f32[144,128]{1,0:T(8,128)S(1)}, f32[144,128]{1,0:T(8,128)S(1)}, u32[]{:S(2)}, u32[]{:S(2)}) %collective-permute-start.6) | collective-permute-done | bytes 73760 | tf_op jit(solution)/shard_map/ppermute | solution.py:486
  21.6 7.9 %collective-permute-start.7 = (f32[224,128]{1,0:T(8,128)S(1)}, f32[224,128]{1,0:T(8,128)S(1)}, u32[]{:S(2)}, u32[]{:S(2)}) collective-permute-start(f32[224,128]{1,0:T(8,128)S(1)} %pack.1.anchor_ref.pack_ref), channel_id=1, source_target_pairs={{1,2},{2,1},{3,4},{4,3},{5,6},{6,5},{7,8},{8,7},{9,10},{10,9},{11,... | collective-permute-start | bytes 344072 | tf_op jit(solution)/shard_map/ppermute | solution.py:479
  29.5 1.6 %tables.1 = (s32[64,128]{1,0:T(8,128)S(1)}, bf16[128,1024]{1,0:T(8,128)(2,1)S(1)}, s32[1,1]{1,0:T(1,128)}, s32[1,1]{1,0:T(1,128)}) custom-call(s32[4096]{0:T(1024)S(1)} %copy-done, f32[224,128]{1,0:T(8,128)S(1)} %pack.1.anchor_ref.pack_ref), custom_call_target="tpu_custom_call" | custom-call | tf_op jit(solution)/shard_map/tables/pallas_call | solution.py:532
  31.1 0.8 %collective-permute-done.7.pair_ref = f32[224,128]{1,0:T(8,128)S(1)} collective-permute-done((f32[224,128]{1,0:T(8,128)S(1)}, f32[224,128]{1,0:T(8,128)S(1)}, u32[]{:S(2)}, u32[]{:S(2)}) %collective-permute-start.7) | collective-permute-done | bytes 114720 | tf_op jit(solution)/shard_map/ppermute | solution.py:479
  32.0 1.9 %collective-permute-start.8 = (f32[224,128]{1,0:T(8,128)S(1)}, f32[224,128]{1,0:T(8,128)S(1)}, u32[]{:S(2)}, u32[]{:S(2)}) collective-permute-start(f32[224,128]{1,0:T(8,128)S(1)} %forward.1), channel_id=1, source_target_pairs={{255,251},{0,4},{1,6},{6,1},{3,8},{8,3},{5,10},{10,5},{7,12},{12,7... | collective-permute-start | bytes 344072 | tf_op jit(solution)/shard_map/ppermute | solution.py:544
  33.9 7.2 %collective-permute-done.8.beyond_ref = f32[224,128]{1,0:T(8,128)S(1)} collective-permute-done((f32[224,128]{1,0:T(8,128)S(1)}, f32[224,128]{1,0:T(8,128)S(1)}, u32[]{:S(2)}, u32[]{:S(2)}) %collective-permute-start.8) | collective-permute-done | bytes 114720 | tf_op jit(solution)/shard_map/ppermute | solution.py:544
  41.1 0.1 collective-permute-start.9
  41.2 1.4 %collective-permute-done.9.there_ref = f32[368,128]{1,0:T(8,128)S(1)} collective-permute-done((f32[368,128]{1,0:T(8,128)S(1)}, f32[368,128]{1,0:T(8,128)S(1)}, u32[]{:S(2)}, u32[]{:S(2)}) %collective-permute-start.9) | collective-permute-done | bytes 188448 | tf_op jit(solution)/shard_map/ppermute | solution.py:486
  42.6 2.0 %window.1 = (f32[128,128]{1,0:T(8,128)S(1)}, f32[64,128]{1,0:T(8,128)S(1)}, f32[32,128]{1,0:T(8,128)S(1)}, f32[64,128]{1,0:T(8,128)S(1)}, f32[64,128]{1,0:T(8,128)}) custom-call(s32[64,128]{1,0:T(8,128)S(1)} %get-tuple-element.128.anchor_ref.phase_ref, f32[224,128]{1,0:T(8,128)S(1)} %pack.1.anchor_ref.pack_ref, f32[368,128]{1,0:T(8,128)S(1)} %side.1.here_ref, ...), custom_call_target="tpu_custom_call" | custom-call | tf_op jit(solution)/shard_map/window/pallas_call | solution.py:546
  44.7 0.0 copy-start.1
  44.7 0.0 copy-start.2
  44.7 0.7 %while.15 = (s32[1,1]{1,0:T(1,128)}, f32[128,128]{1,0:T(8,128)S(1)}, f32[64,128]{1,0:T(8,128)S(1)}, f32[64,128]{1,0:T(8,128)S(1)}, f32[64,128]{1,0:T(8,128)}, /*...) while((s32[1,1]{1,0:T(1,128)}, f32[128,128]{1,0:T(8,128)S(1)}, f32[64,128]{1,0:T(8,128)S(1)}, ...), condition=%region_1.0_spmd, body=%region_0.0_spmd | while | flops 1 | bytes 590025 | solution.py:564
  45.4 3.5 %spatial.1 = (bf16[32,32,128]{2,1,0:T(8,128)(2,1)S(1)}, bf16[32,32,128]{2,1,0:T(8,128)(2,1)S(1)}) custom-call(s32[4096]{0:T(1024)S(1)} %copy-done, bf16[128,1024]{1,0:T(8,128)(2,1)S(1)} %get-tuple-element.87.repeat_ref, bf16[1024,512]{1,0:T(8,128)(2,1)S(1)} %get-tuple-element.88.refs_0_, bf16[1024,512]{1,0:T(8,128)(2,1)S(1)} %get-tuple-element.89.refs_1_, ...), custom_call_target="tpu_custom_call" | custom-call | tf_op jit(solution)/shard_map/spatial/pallas_call | solution.py:566
  48.9 7.9 %collective-permute-start.10 = (bf16[32,32,128]{2,1,0:T(8,128)(2,1)S(1)}, bf16[32,32,128]{2,1,0:T(8,128)(2,1)S(1)}, u32[]{:S(2)}, u32[]{:S(2)}) collective-permute-start(bf16[32,32,128]{2,1,0:T(8,128)(2,1)S(1)} %get-tuple-element.97), channel_id=1, source_target_pairs={{1,2},{2,1},{3,4},{4,3},{5,6},{6,5},{7,8},{8,7},{9,10},{10,9},{11,... | collective-permute-start | bytes 786440 | tf_op jit(solution)/shard_map/ppermute | solution.py:479
  56.8 1.5 %traces.1 = (f32[32,64]{1,0:T(8,128)}, bf16[32,32,128]{2,1,0:T(8,128)(2,1)S(1)}) custom-call(s32[4096]{0:T(1024)S(1)} %copy-done, f32[128,128]{1,0:T(8,128)S(1)} %get-tuple-element.86.refs_5_.state_ref, bf16[32,32,128]{2,1,0:T(8,128)(2,1)S(1)} %get-tuple-element.94.own_ref), custom_call_target="tpu_custom_call" | custom-call | tf_op jit(solution)/shard_map/traces/pallas_call | solution.py:580
  58.3 0.0 collective-permute-start.11
  58.3 2.5 %collective-permute-done.10.recv_ref = bf16[32,32,128]{2,1,0:T(8,128)(2,1)S(1)} collective-permute-done((bf16[32,32,128]{2,1,0:T(8,128)(2,1)S(1)}, bf16[32,32,128]{2,1,0:T(8,128)(2,1)S(1)}, u32[]{:S(2)}, u32[]{:S(2)}) %collective-permute-start.10) | collective-permute-done | bytes 262176 | tf_op jit(solution)/shard_map/ppermute | solution.py:479
  60.8 0.0 collective-permute-start.12
  60.8 0.0 collective-permute-done.11.sib_own_ref
  60.8 1.5 %collective-permute-done.12.sib_recv_ref = bf16[32,32,128]{2,1,0:T(8,128)(2,1)S(1)} collective-permute-done((bf16[32,32,128]{2,1,0:T(8,128)(2,1)S(1)}, bf16[32,32,128]{2,1,0:T(8,128)(2,1)S(1)}, u32[]{:S(2)}, u32[]{:S(2)}) %collective-permute-start.12) | collective-permute-done | bytes 262176 | tf_op jit(solution)/shard_map/ppermute | solution.py:486
  62.3 0.0 copy-done.1
  62.3 0.0 copy-done.2
  62.3 2.1 %patches.1 = bf16[32,64,64]{2,1,0:T(8,128)(2,1)} custom-call(s32[32]{0:T(128)S(1)} %copy-done.1, s32[32]{0:T(128)S(1)} %copy-done.2, bf16[32,32,128]{2,1,0:T(8,128)(2,1)S(1)} %get-tuple-element.96.own_ref, bf16[32,32,128]{2,1,0:T(8,128)(2,1)S(1)} %collective-permute-done.10.recv_ref, bf16[32,32,128]{2,1,0:T(8,128)(2,1)S(1)} %collective-permute-done.11.sib_own_ref, ...), custom_call_target="tpu_custom_call" | custom-call | tf_op jit(solution)/shard_map/patches/pallas_call | solution.py:591
  (3 shorter events, 0.0 us)
Async XLA Ops:
  0.6 17.0 %copy-start = (s32[4096]{0:T(1024)S(1)}, s32[4096]{0:T(1024)}, u32[]{:S(2)}) copy-start(s32[4096]{0:T(1024)} %colour_ref.7) | copy-start | bytes 49156
  0.6 17.0 %collective-permute-start.4 = (bf16[64,64,512]{2,1,0:T(8,128)(2,1)}, bf16[64,64,512]{2,1,0:T(8,128)(2,1)S(1)}, u32[]{:S(2)}, u32[]{:S(2)}) collective-permute-start(bf16[64,64,512]{2,1,0:T(8,128)(2,1)} %movie_ref.1), channel_id=1, source_target_pairs={{0,1},{1,0},{2,3},{3,2},{4,5},{5,4},{6,7},{7,6},{8,9},{9,8},{10,11... | collective-permute-start | bytes 12582920 | tf_op jit(solution)/shard_map/ppermute | solution.py:486
  2.9 14.7 %collective-permute-start.5 = (bf16[32,32,128]{2,1,0:T(8,128)(2,1)S(1)}, bf16[32,32,128]{2,1,0:T(8,128)(2,1)S(1)}, u32[]{:S(2)}, u32[]{:S(2)}) collective-permute-start(bf16[32,32,128]{2,1,0:T(8,128)(2,1)S(1)} %get-tuple-element.74), channel_id=1, source_target_pairs={{1,2},{2,1},{3,4},{4,3},{5,6},{6,5},{7,8},{8,7},{9,10},{10,9},{11,... | collective-permute-start | bytes 786440 | tf_op jit(solution)/shard_map/ppermute | solution.py:479
  13.6 1.5 %collective-permute-start.3 = (f32[32,64]{1,0:T(8,128)}, f32[32,64]{1,0:T(8,128)S(1)}, u32[]{:S(2)}, u32[]{:S(2)}) collective-permute-start(f32[32,64]{1,0:T(8,128)} %traces_ref.1), channel_id=1, source_target_pairs={{0,1},{1,0},{2,3},{3,2},{4,5},{5,4},{6,7},{7,6},{8,9},{9,8},{10,11... | collective-permute-start | bytes 24584 | tf_op jit(solution)/shard_map/ppermute | solution.py:486
  20.3 1.3 %collective-permute-start.6 = (f32[144,128]{1,0:T(8,128)S(1)}, f32[144,128]{1,0:T(8,128)S(1)}, u32[]{:S(2)}, u32[]{:S(2)}) collective-permute-start(f32[144,128]{1,0:T(8,128)S(1)} %get-tuple-element.77.mine_ref), channel_id=1, source_target_pairs={{0,1},{1,0},{2,3},{3,2},{4,5},{5,4},{6,7},{7,6},{8,9},{9,8},{10,11... | collective-permute-start | bytes 221192 | tf_op jit(solution)/shard_map/ppermute | solution.py:486
  21.6 10.3 %collective-permute-start.7 = (f32[224,128]{1,0:T(8,128)S(1)}, f32[224,128]{1,0:T(8,128)S(1)}, u32[]{:S(2)}, u32[]{:S(2)}) collective-permute-start(f32[224,128]{1,0:T(8,128)S(1)} %pack.1.anchor_ref.pack_ref), channel_id=1, source_target_pairs={{1,2},{2,1},{3,4},{4,3},{5,6},{6,5},{7,8},{8,7},{9,10},{10,9},{11,... | collective-permute-start | bytes 344072 | tf_op jit(solution)/shard_map/ppermute | solution.py:479
  32.0 9.1 %collective-permute-start.8 = (f32[224,128]{1,0:T(8,128)S(1)}, f32[224,128]{1,0:T(8,128)S(1)}, u32[]{:S(2)}, u32[]{:S(2)}) collective-permute-start(f32[224,128]{1,0:T(8,128)S(1)} %forward.1), channel_id=1, source_target_pairs={{255,251},{0,4},{1,6},{6,1},{3,8},{8,3},{5,10},{10,5},{7,12},{12,7... | collective-permute-start | bytes 344072 | tf_op jit(solution)/shard_map/ppermute | solution.py:544
  41.1 1.5 %collective-permute-start.9 = (f32[368,128]{1,0:T(8,128)S(1)}, f32[368,128]{1,0:T(8,128)S(1)}, u32[]{:S(2)}, u32[]{:S(2)}) collective-permute-start(f32[368,128]{1,0:T(8,128)S(1)} %side.1.here_ref), channel_id=1, source_target_pairs={{0,1},{1,0},{2,3},{3,2},{4,5},{5,4},{6,7},{7,6},{8,9},{9,8},{10,11... | collective-permute-start | bytes 565256 | tf_op jit(solution)/shard_map/ppermute | solution.py:486
  44.7 17.7 %copy-start.1 = (s32[32]{0:T(128)S(1)}, s32[32]{0:T(128)}, u32[]{:S(2)}) copy-start(s32[32]{0:T(128)} %rows_ref.3) | copy-start | bytes 388
  44.7 17.7 %copy-start.2 = (s32[32]{0:T(128)S(1)}, s32[32]{0:T(128)}, u32[]{:S(2)}) copy-start(s32[32]{0:T(128)} %cols_ref.3) | copy-start | bytes 388
  48.9 11.9 %collective-permute-start.10 = (bf16[32,32,128]{2,1,0:T(8,128)(2,1)S(1)}, bf16[32,32,128]{2,1,0:T(8,128)(2,1)S(1)}, u32[]{:S(2)}, u32[]{:S(2)}) collective-permute-start(bf16[32,32,128]{2,1,0:T(8,128)(2,1)S(1)} %get-tuple-element.97), channel_id=1, source_target_pairs={{1,2},{2,1},{3,4},{4,3},{5,6},{6,5},{7,8},{8,7},{9,10},{10,9},{11,... | collective-permute-start | bytes 786440 | tf_op jit(solution)/shard_map/ppermute | solution.py:479
  58.3 2.5 %collective-permute-start.11 = (bf16[32,32,128]{2,1,0:T(8,128)(2,1)S(1)}, bf16[32,32,128]{2,1,0:T(8,128)(2,1)S(1)}, u32[]{:S(2)}, u32[]{:S(2)}) collective-permute-start(bf16[32,32,128]{2,1,0:T(8,128)(2,1)S(1)} %get-tuple-element.96.own_ref), channel_id=1, source_target_pairs={{0,1},{1,0},{2,3},{3,2},{4,5},{5,4},{6,7},{7,6},{8,9},{9,8},{10,11... | collective-permute-start | bytes 786440 | tf_op jit(solution)/shard_map/ppermute | solution.py:486
  60.8 1.5 %collective-permute-start.12 = (bf16[32,32,128]{2,1,0:T(8,128)(2,1)S(1)}, bf16[32,32,128]{2,1,0:T(8,128)(2,1)S(1)}, u32[]{:S(2)}, u32[]{:S(2)}) collective-permute-start(bf16[32,32,128]{2,1,0:T(8,128)(2,1)S(1)} %collective-permute-done.10.recv_ref), channel_id=1, source_target_pairs={{0,1},{1,0},{2,3},{3,2},{4,5},{5,4},{6,7},{7,6},{8,9},{9,8},{10,11... | collective-permute-start | bytes 786440 | tf_op jit(solution)/shard_map/ppermute | solution.py:486

commit v3 on v2

--- a/solution.py
+++ b/solution.py
@@ -414,7 +414,7 @@
             states[g] = fresh.astype(f32)
         return carry
 
-    lax.fori_loop(0, 2 * BINS, update, 0)
+    lax.fori_loop(0, 2 * BINS, update, 0, unroll=2)
     for s in range(SLOTS):
         first = (s // LAYERS) * COLOURS
         own_ref[s] = state_ref[first + colour_ref[tile * SLOTS + s]]

time: 65.1 us -> 65.1 us (level)
  no operation moved by 1% of the time
where the time goes in v3:
time: 65.1 us; the launch traced here: 64.5 us
  starting transfers between devices  28.6 us (44%)
  Pallas kernels  18.1 us (28%)
  waiting for transfers between devices  16.4 us (25%)
  between operations  0.76 us (1%)
  loops' own time  0.68 us (1%)
    ppermute x3, starting transfers between devices, pair_swap(): return lax.ppermute(value, ('tile', 'frame'), swap_pairs)  26.3 us
    ppermute x1, waiting for transfers between devices, on_device(): beyond = lax.ppermute(onward, ('tile', 'frame'), far_pairs)  7.19 us
    ppermute x6, waiting for transfers between devices, chip_swap(): return lax.ppermute(value, 'frame', [(0, 1), (1, 0)])  5.58 us
    ppermute x3, waiting for transfers between devices, pair_swap(): return lax.ppermute(value, ('tile', 'frame'), swap_pairs)  3.63 us
    pallas_call x1, Pallas kernels, on_device(): call(functools.partial(spatial_kernel, tiles), [smem] + [vmem] * 8, [piec...  3.54 us
    pallas_call x1, Pallas kernels, on_device(): call(functools.partial(partial_kernel, tiles), [smem] + [vmem] * 6, [shap...  2.72 us
    pallas_call x1, Pallas kernels, on_device(): call(fetch_kernel, [smem, vmem, vmem, hbm], [shape((SLOTS, 64)), shape((S...  2.3 us
    pallas_call x1, Pallas kernels, on_device(): call(slab_kernel, [smem, smem, smem, hbm], [piece, piece], 'slabs', 8, [p...  2.18 us
  transfers between devices with their start and end apart: 10, of which 8 were waited for; matrix products, arithmetic and copies ran while one was open for 0% of the time, Pallas kernels for 12%

profile of v3, /device:TPU:6, one launch (start us, length us, event | category | flops | bytes accessed | tf_op | source)
XLA Modules:
  0.0 64.5 jit_solution(12018384888405976893)
XLA Ops:
  0.6 0.0 copy-start
  0.6 0.1 collective-permute-start.4
  0.7 2.2 %slabs.1 = (bf16[32,32,128]{2,1,0:T(8,128)(2,1)S(1)}, bf16[32,32,128]{2,1,0:T(8,128)(2,1)S(1)}) custom-call(s32[32]{0:T(128)} %rows_ref.3, s32[32]{0:T(128)} %cols_ref.3, s32[32]{0:T(128)} %live_ref.3, bf16[32,64,64]{2,1,0:T(8,128)(2,1)} %patches_ref.1), custom_call_target="tpu_custom_call" | custom-call | tf_op jit(solution)/shard_map/slabs/pallas_call | solution.py:496
  2.9 10.6 %collective-permute-start.5 = (bf16[32,32,128]{2,1,0:T(8,128)(2,1)S(1)}, bf16[32,32,128]{2,1,0:T(8,128)(2,1)S(1)}, u32[]{:S(2)}, u32[]{:S(2)}) collective-permute-start(bf16[32,32,128]{2,1,0:T(8,128)(2,1)S(1)} %get-tuple-element.74), channel_id=1, source_target_pairs={{1,2},{2,1},{3,4},{4,3},{5,6},{6,5},{7,8},{8,7},{9,10},{10,9},{11,... | collective-permute-start | bytes 786440 | tf_op jit(solution)/shard_map/ppermute | solution.py:479
  13.6 0.1 collective-permute-start.3
  13.7 1.4 %collective-permute-done.3.far_ref = f32[32,64]{1,0:T(8,128)S(1)} collective-permute-done((f32[32,64]{1,0:T(8,128)}, f32[32,64]{1,0:T(8,128)S(1)}, u32[]{:S(2)}, u32[]{:S(2)}) %collective-permute-start.3) | collective-permute-done | bytes 8224 | tf_op jit(solution)/shard_map/ppermute | solution.py:486
  15.0 2.3 %fetch.1 = (f32[32,64]{1,0:T(8,128)S(1)}, f32[32,64]{1,0:T(8,128)S(1)}, bf16[64,32,512]{2,1,0:T(8,128)(2,1)S(1)}) custom-call(s32[32]{0:T(128)} %live_ref.3, f32[32,64]{1,0:T(8,128)} %traces_ref.1, f32[32,64]{1,0:T(8,128)S(1)} %collective-permute-done.3.far_ref, bf16[64,64,512]{2,1,0:T(8,128)(2,1)} %movie_ref.1), custom_call_target="tpu_custom_call" | custom-call | tf_op jit(solution)/shard_map/fetch/pallas_call | solution.py:509
  17.3 0.2 collective-permute-done.5.recv_ref
  17.6 0.0 collective-permute-done.4.other_ref
  17.6 0.0 copy-done
  17.6 2.7 %partial_sums.1 = (bf16[64,32,128]{2,1,0:T(8,128)(2,1)S(1)}, f32[144,128]{1,0:T(8,128)S(1)}, bf16[1024,512]{1,0:T(8,128)(2,1)S(1)}, bf16[1024,512]{1,0:T(8,128)(...) custom-call(s32[4096]{0:T(1024)S(1)} %copy-done, ...), custom_call_target="tpu_custom_call" | custom-call | tf_op jit(solution)/shard_map/partial_sums/pallas_call | solution.py:518
  20.3 0.0 collective-permute-start.6
  20.3 1.3 %collective-permute-done.6.far_ref = f32[144,128]{1,0:T(8,128)S(1)} collective-permute-done((f32[144,128]{1,0:T(8,128)S(1)}, f32[144,128]{1,0:T(8,128)S(1)}, u32[]{:S(2)}, u32[]{:S(2)}) %collective-permute-start.6) | collective-permute-done | bytes 73760 | tf_op jit(solution)/shard_map/ppermute | solution.py:486
  21.6 7.9 %collective-permute-start.7 = (f32[224,128]{1,0:T(8,128)S(1)}, f32[224,128]{1,0:T(8,128)S(1)}, u32[]{:S(2)}, u32[]{:S(2)}) collective-permute-start(f32[224,128]{1,0:T(8,128)S(1)} %pack.1.anchor_ref.pack_ref), channel_id=1, source_target_pairs={{1,2},{2,1},{3,4},{4,3},{5,6},{6,5},{7,8},{8,7},{9,10},{10,9},{11,... | collective-permute-start | bytes 344072 | tf_op jit(solution)/shard_map/ppermute | solution.py:479
  29.5 1.6 %tables.1 = (s32[64,128]{1,0:T(8,128)S(1)}, bf16[128,1024]{1,0:T(8,128)(2,1)S(1)}, s32[1,1]{1,0:T(1,128)}, s32[1,1]{1,0:T(1,128)}) custom-call(s32[4096]{0:T(1024)S(1)} %copy-done, f32[224,128]{1,0:T(8,128)S(1)} %pack.1.anchor_ref.pack_ref), custom_call_target="tpu_custom_call" | custom-call | tf_op jit(solution)/shard_map/tables/pallas_call | solution.py:532
  31.1 0.8 %collective-permute-done.7.pair_ref = f32[224,128]{1,0:T(8,128)S(1)} collective-permute-done((f32[224,128]{1,0:T(8,128)S(1)}, f32[224,128]{1,0:T(8,128)S(1)}, u32[]{:S(2)}, u32[]{:S(2)}) %collective-permute-start.7) | collective-permute-done | bytes 114720 | tf_op jit(solution)/shard_map/ppermute | solution.py:479
  32.0 1.9 %collective-permute-start.8 = (f32[224,128]{1,0:T(8,128)S(1)}, f32[224,128]{1,0:T(8,128)S(1)}, u32[]{:S(2)}, u32[]{:S(2)}) collective-permute-start(f32[224,128]{1,0:T(8,128)S(1)} %forward.1), channel_id=1, source_target_pairs={{255,251},{0,4},{1,6},{6,1},{3,8},{8,3},{5,10},{10,5},{7,12},{12,7... | collective-permute-start | bytes 344072 | tf_op jit(solution)/shard_map/ppermute | solution.py:544
  33.9 7.2 %collective-permute-done.8.beyond_ref = f32[224,128]{1,0:T(8,128)S(1)} collective-permute-done((f32[224,128]{1,0:T(8,128)S(1)}, f32[224,128]{1,0:T(8,128)S(1)}, u32[]{:S(2)}, u32[]{:S(2)}) %collective-permute-start.8) | collective-permute-done | bytes 114720 | tf_op jit(solution)/shard_map/ppermute | solution.py:544
  41.1 0.1 collective-permute-start.9
  41.2 1.4 %collective-permute-done.9.there_ref = f32[368,128]{1,0:T(8,128)S(1)} collective-permute-done((f32[368,128]{1,0:T(8,128)S(1)}, f32[368,128]{1,0:T(8,128)S(1)}, u32[]{:S(2)}, u32[]{:S(2)}) %collective-permute-start.9) | collective-permute-done | bytes 188448 | tf_op jit(solution)/shard_map/ppermute | solution.py:486
  42.6 2.0 %window.1 = (f32[128,128]{1,0:T(8,128)S(1)}, f32[64,128]{1,0:T(8,128)S(1)}, f32[32,128]{1,0:T(8,128)S(1)}, f32[64,128]{1,0:T(8,128)S(1)}, f32[64,128]{1,0:T(8,128)}) custom-call(s32[64,128]{1,0:T(8,128)S(1)} %get-tuple-element.128.anchor_ref.phase_ref, f32[224,128]{1,0:T(8,128)S(1)} %pack.1.anchor_ref.pack_ref, f32[368,128]{1,0:T(8,128)S(1)} %side.1.here_ref, ...), custom_call_target="tpu_custom_call" | custom-call | tf_op jit(solution)/shard_map/window/pallas_call | solution.py:546
  44.7 0.0 copy-start.1
  44.7 0.0 copy-start.2
  44.7 0.7 %while.15 = (s32[1,1]{1,0:T(1,128)}, f32[128,128]{1,0:T(8,128)S(1)}, f32[64,128]{1,0:T(8,128)S(1)}, f32[64,128]{1,0:T(8,128)S(1)}, f32[64,128]{1,0:T(8,128)}, /*...) while((s32[1,1]{1,0:T(1,128)}, f32[128,128]{1,0:T(8,128)S(1)}, f32[64,128]{1,0:T(8,128)S(1)}, ...), condition=%region_1.0_spmd, body=%region_0.0_spmd | while | flops 1 | bytes 590025 | solution.py:564
  45.4 3.5 %spatial.1 = (bf16[32,32,128]{2,1,0:T(8,128)(2,1)S(1)}, bf16[32,32,128]{2,1,0:T(8,128)(2,1)S(1)}) custom-call(s32[4096]{0:T(1024)S(1)} %copy-done, bf16[128,1024]{1,0:T(8,128)(2,1)S(1)} %get-tuple-element.87.repeat_ref, bf16[1024,512]{1,0:T(8,128)(2,1)S(1)} %get-tuple-element.88.refs_0_, bf16[1024,512]{1,0:T(8,128)(2,1)S(1)} %get-tuple-element.89.refs_1_, ...), custom_call_target="tpu_custom_call" | custom-call | tf_op jit(solution)/shard_map/spatial/pallas_call | solution.py:566
  48.9 7.9 %collective-permute-start.10 = (bf16[32,32,128]{2,1,0:T(8,128)(2,1)S(1)}, bf16[32,32,128]{2,1,0:T(8,128)(2,1)S(1)}, u32[]{:S(2)}, u32[]{:S(2)}) collective-permute-start(bf16[32,32,128]{2,1,0:T(8,128)(2,1)S(1)} %get-tuple-element.97), channel_id=1, source_target_pairs={{1,2},{2,1},{3,4},{4,3},{5,6},{6,5},{7,8},{8,7},{9,10},{10,9},{11,... | collective-permute-start | bytes 786440 | tf_op jit(solution)/shard_map/ppermute | solution.py:479
  56.8 1.5 %traces.1 = (f32[32,64]{1,0:T(8,128)}, bf16[32,32,128]{2,1,0:T(8,128)(2,1)S(1)}) custom-call(s32[4096]{0:T(1024)S(1)} %copy-done, f32[128,128]{1,0:T(8,128)S(1)} %get-tuple-element.86.refs_5_.state_ref, bf16[32,32,128]{2,1,0:T(8,128)(2,1)S(1)} %get-tuple-element.94.own_ref), custom_call_target="tpu_custom_call" | custom-call | tf_op jit(solution)/shard_map/traces/pallas_call | solution.py:580
  58.3 0.0 collective-permute-start.11
  58.3 2.5 %collective-permute-done.10.recv_ref = bf16[32,32,128]{2,1,0:T(8,128)(2,1)S(1)} collective-permute-done((bf16[32,32,128]{2,1,0:T(8,128)(2,1)S(1)}, bf16[32,32,128]{2,1,0:T(8,128)(2,1)S(1)}, u32[]{:S(2)}, u32[]{:S(2)}) %collective-permute-start.10) | collective-permute-done | bytes 262176 | tf_op jit(solution)/shard_map/ppermute | solution.py:479
  60.8 0.0 collective-permute-start.12
  60.8 0.0 collective-permute-done.11.sib_own_ref
  60.8 1.5 %collective-permute-done.12.sib_recv_ref = bf16[32,32,128]{2,1,0:T(8,128)(2,1)S(1)} collective-permute-done((bf16[32,32,128]{2,1,0:T(8,128)(2,1)S(1)}, bf16[32,32,128]{2,1,0:T(8,128)(2,1)S(1)}, u32[]{:S(2)}, u32[]{:S(2)}) %collective-permute-start.12) | collective-permute-done | bytes 262176 | tf_op jit(solution)/shard_map/ppermute | solution.py:486
  62.3 0.0 copy-done.1
  62.4 0.0 copy-done.2
  62.4 2.1 %patches.1 = bf16[32,64,64]{2,1,0:T(8,128)(2,1)} custom-call(s32[32]{0:T(128)S(1)} %copy-done.1, s32[32]{0:T(128)S(1)} %copy-done.2, bf16[32,32,128]{2,1,0:T(8,128)(2,1)S(1)} %get-tuple-element.96.own_ref, bf16[32,32,128]{2,1,0:T(8,128)(2,1)S(1)} %collective-permute-done.10.recv_ref, bf16[32,32,128]{2,1,0:T(8,128)(2,1)S(1)} %collective-permute-done.11.sib_own_ref, ...), custom_call_target="tpu_custom_call" | custom-call | tf_op jit(solution)/shard_map/patches/pallas_call | solution.py:591
  (3 shorter events, 0.0 us)
Async XLA Ops:
  0.6 17.0 %copy-start = (s32[4096]{0:T(1024)S(1)}, s32[4096]{0:T(1024)}, u32[]{:S(2)}) copy-start(s32[4096]{0:T(1024)} %colour_ref.7) | copy-start | bytes 49156
  0.6 17.0 %collective-permute-start.4 = (bf16[64,64,512]{2,1,0:T(8,128)(2,1)}, bf16[64,64,512]{2,1,0:T(8,128)(2,1)S(1)}, u32[]{:S(2)}, u32[]{:S(2)}) collective-permute-start(bf16[64,64,512]{2,1,0:T(8,128)(2,1)} %movie_ref.1), channel_id=1, source_target_pairs={{0,1},{1,0},{2,3},{3,2},{4,5},{5,4},{6,7},{7,6},{8,9},{9,8},{10,11... | collective-permute-start | bytes 12582920 | tf_op jit(solution)/shard_map/ppermute | solution.py:486
  2.9 14.7 %collective-permute-start.5 = (bf16[32,32,128]{2,1,0:T(8,128)(2,1)S(1)}, bf16[32,32,128]{2,1,0:T(8,128)(2,1)S(1)}, u32[]{:S(2)}, u32[]{:S(2)}) collective-permute-start(bf16[32,32,128]{2,1,0:T(8,128)(2,1)S(1)} %get-tuple-element.74), channel_id=1, source_target_pairs={{1,2},{2,1},{3,4},{4,3},{5,6},{6,5},{7,8},{8,7},{9,10},{10,9},{11,... | collective-permute-start | bytes 786440 | tf_op jit(solution)/shard_map/ppermute | solution.py:479
  13.6 1.5 %collective-permute-start.3 = (f32[32,64]{1,0:T(8,128)}, f32[32,64]{1,0:T(8,128)S(1)}, u32[]{:S(2)}, u32[]{:S(2)}) collective-permute-start(f32[32,64]{1,0:T(8,128)} %traces_ref.1), channel_id=1, source_target_pairs={{0,1},{1,0},{2,3},{3,2},{4,5},{5,4},{6,7},{7,6},{8,9},{9,8},{10,11... | collective-permute-start | bytes 24584 | tf_op jit(solution)/shard_map/ppermute | solution.py:486
  20.3 1.3 %collective-permute-start.6 = (f32[144,128]{1,0:T(8,128)S(1)}, f32[144,128]{1,0:T(8,128)S(1)}, u32[]{:S(2)}, u32[]{:S(2)}) collective-permute-start(f32[144,128]{1,0:T(8,128)S(1)} %get-tuple-element.77.mine_ref), channel_id=1, source_target_pairs={{0,1},{1,0},{2,3},{3,2},{4,5},{5,4},{6,7},{7,6},{8,9},{9,8},{10,11... | collective-permute-start | bytes 221192 | tf_op jit(solution)/shard_map/ppermute | solution.py:486
  21.6 10.3 %collective-permute-start.7 = (f32[224,128]{1,0:T(8,128)S(1)}, f32[224,128]{1,0:T(8,128)S(1)}, u32[]{:S(2)}, u32[]{:S(2)}) collective-permute-start(f32[224,128]{1,0:T(8,128)S(1)} %pack.1.anchor_ref.pack_ref), channel_id=1, source_target_pairs={{1,2},{2,1},{3,4},{4,3},{5,6},{6,5},{7,8},{8,7},{9,10},{10,9},{11,... | collective-permute-start | bytes 344072 | tf_op jit(solution)/shard_map/ppermute | solution.py:479
  32.0 9.1 %collective-permute-start.8 = (f32[224,128]{1,0:T(8,128)S(1)}, f32[224,128]{1,0:T(8,128)S(1)}, u32[]{:S(2)}, u32[]{:S(2)}) collective-permute-start(f32[224,128]{1,0:T(8,128)S(1)} %forward.1), channel_id=1, source_target_pairs={{255,251},{0,4},{1,6},{6,1},{3,8},{8,3},{5,10},{10,5},{7,12},{12,7... | collective-permute-start | bytes 344072 | tf_op jit(solution)/shard_map/ppermute | solution.py:544
  41.1 1.5 %collective-permute-start.9 = (f32[368,128]{1,0:T(8,128)S(1)}, f32[368,128]{1,0:T(8,128)S(1)}, u32[]{:S(2)}, u32[]{:S(2)}) collective-permute-start(f32[368,128]{1,0:T(8,128)S(1)} %side.1.here_ref), channel_id=1, source_target_pairs={{0,1},{1,0},{2,3},{3,2},{4,5},{5,4},{6,7},{7,6},{8,9},{9,8},{10,11... | collective-permute-start | bytes 565256 | tf_op jit(solution)/shard_map/ppermute | solution.py:486
  44.7 17.7 %copy-start.1 = (s32[32]{0:T(128)S(1)}, s32[32]{0:T(128)}, u32[]{:S(2)}) copy-start(s32[32]{0:T(128)} %rows_ref.3) | copy-start | bytes 388
  44.7 17.7 %copy-start.2 = (s32[32]{0:T(128)S(1)}, s32[32]{0:T(128)}, u32[]{:S(2)}) copy-start(s32[32]{0:T(128)} %cols_ref.3) | copy-start | bytes 388
  48.9 11.9 %collective-permute-start.10 = (bf16[32,32,128]{2,1,0:T(8,128)(2,1)S(1)}, bf16[32,32,128]{2,1,0:T(8,128)(2,1)S(1)}, u32[]{:S(2)}, u32[]{:S(2)}) collective-permute-start(bf16[32,32,128]{2,1,0:T(8,128)(2,1)S(1)} %get-tuple-element.97), channel_id=1, source_target_pairs={{1,2},{2,1},{3,4},{4,3},{5,6},{6,5},{7,8},{8,7},{9,10},{10,9},{11,... | collective-permute-start | bytes 786440 | tf_op jit(solution)/shard_map/ppermute | solution.py:479
  58.3 2.5 %collective-permute-start.11 = (bf16[32,32,128]{2,1,0:T(8,128)(2,1)S(1)}, bf16[32,32,128]{2,1,0:T(8,128)(2,1)S(1)}, u32[]{:S(2)}, u32[]{:S(2)}) collective-permute-start(bf16[32,32,128]{2,1,0:T(8,128)(2,1)S(1)} %get-tuple-element.96.own_ref), channel_id=1, source_target_pairs={{0,1},{1,0},{2,3},{3,2},{4,5},{5,4},{6,7},{7,6},{8,9},{9,8},{10,11... | collective-permute-start | bytes 786440 | tf_op jit(solution)/shard_map/ppermute | solution.py:486
  60.8 1.5 %collective-permute-start.12 = (bf16[32,32,128]{2,1,0:T(8,128)(2,1)S(1)}, bf16[32,32,128]{2,1,0:T(8,128)(2,1)S(1)}, u32[]{:S(2)}, u32[]{:S(2)}) collective-permute-start(bf16[32,32,128]{2,1,0:T(8,128)(2,1)S(1)} %collective-permute-done.10.recv_ref), channel_id=1, source_target_pairs={{0,1},{1,0},{2,3},{3,2},{4,5},{5,4},{6,7},{7,6},{8,9},{9,8},{10,11... | collective-permute-start | bytes 786440 | tf_op jit(solution)/shard_map/ppermute | solution.py:486
